TPU v7x, 768 devices: a whole 4x8x12 slice. The times are simulated.
768 devices in a mesh: ctx: 16 (over y_hi, x), sub: 48 (over z, y_lo, core).
Axes of the slice: x: 4, y: 8 (y_hi: 4, y_lo: 2; y = y_hi * 2 + y_lo), z: 12, core: 2. Of those that a mesh axis runs over, the one named last changes fastest.
Arguments:
- queries: bfloat16 [98304, 8, 128], P(('ctx', 'sub')), may hold values from -52 to 52
- key_rows: bfloat16 [98304, 128], P(('ctx', 'sub')), may hold values from -5 to 5
- value_rows: bfloat16 [98304, 128], P(('ctx', 'sub')), may hold values from -6 to 6
- block_docs: int32 [768], replicated, may hold values from 0 to 3, never falling along the last dimension, each value on 1 to 384 neighbouring positions
- windows: int32 [8], replicated, may hold values from 1 to 32, as said below
Outputs:
- attended: bfloat16 [98304, 8, 128], P(('ctx', 'sub'))
Inputs may be any that keep to these rules, and one draw needn't show every extreme that they name: `windows`: some head's window is exactly 32 blocks.
All inputs are finite; a program needn't handle non-finite values.
Results may differ from a plain program's by a relative error of at most 0.0044.
Values may be sent and summed in bfloat16 or wider, within the bound.
A program may use at most 64 MiB of HBM per device.

v0:
```python
import math

import jax
import jax.numpy as jnp
from jax import lax
from jax.sharding import PartitionSpec as P

BLK = 128
WMAX = 32


def from_behind(value, axis, steps):
    count = lax.axis_size(axis)
    initial, last = (max(0, -steps), min(count, count - steps))
    return lax.ppermute(value, axis, [(source, source + steps) for source in range(initial, last)])


def lookup_docs(blocks, block_docs):
    block_index = jnp.arange(block_docs.shape[0], dtype=jnp.int32)
    matches = blocks[:, None] == block_index[None, :]
    return jnp.sum(jnp.where(matches, block_docs[None, :], 0), axis=1)


def visible(query_places, key_places, block_docs, windows, block_size):
    query_blocks = query_places // block_size
    key_blocks = key_places // block_size
    same_doc = (
        lookup_docs(query_blocks, block_docs)[:, None]
        == lookup_docs(key_blocks, block_docs)[None, :]
    )
    ordered = (key_places[None, :] <= query_places[:, None]) & (key_places[None, :] >= 0)
    in_window = (query_blocks[:, None] - key_blocks[None, :])[:, None, :] < windows[None, :, None]
    return (same_doc & ordered)[:, None, :] & in_window


def scores(query_rows, key_part):
    product = jnp.einsum("qhd,kd->qhk", query_rows, key_part, preferred_element_type=jnp.float32)
    return product * query_rows.shape[-1] ** (-0.5)


def masked_logits(query_rows, query_places, stacked, key_places, block_docs, windows, block_size):

    def masked_visit_piece(highest, element):
        portion, places = element
        allowed = visible(query_places, places, block_docs, windows, block_size)
        logits = jnp.where(allowed, scores(query_rows, portion[0]), -jnp.inf)
        return (jnp.maximum(highest, jnp.max(logits, axis=2)), logits)

    initial = jnp.full(query_rows.shape[:2], -jnp.inf, jnp.float32)
    return lax.scan(masked_visit_piece, initial, (stacked, key_places))


def row_sums(query_rows, highest, stored, value_pieces):

    def row_visit_piece(totals, element):
        logits, values = element
        weights = jnp.exp(logits - highest[:, :, None]).astype(jnp.bfloat16)
        numerator = totals[0] + jnp.einsum(
            "qhk,kd->qhd", weights, values, preferred_element_type=jnp.float32
        )
        denominator = totals[1] + jnp.sum(weights.astype(jnp.float32), axis=2)
        return ((numerator, denominator), None)

    initial = (
        jnp.zeros(query_rows.shape, jnp.float32),
        jnp.zeros(query_rows.shape[:2], jnp.float32),
    )
    totals, unused = lax.scan(row_visit_piece, initial, (stored, value_pieces))
    return totals


def local(queries, key_rows, value_rows, block_docs, windows):
    block_size = BLK
    local_rows = queries.shape[0]
    head_size = key_rows.shape[1]
    ctx_count = lax.axis_size("ctx")
    sub_count = lax.axis_size("sub")
    ctx_place = lax.axis_index("ctx")
    sub_place = lax.axis_index("sub")
    shard_len = local_rows * sub_count
    span = WMAX * BLK
    first_row = (ctx_place * sub_count + sub_place) * local_rows
    paired = jnp.stack([key_rows, value_rows])
    whole = lax.all_gather(paired, "sub", axis=1, tiled=True)
    reach_shards = min(ctx_count - 1, (span + shard_len - 1) // shard_len)

    def retreat(carried, unused):
        arrived = from_behind(carried, "ctx", 1)
        return (arrived, arrived)

    earlier = lax.scan(retreat, whole, None, length=reach_shards)[1]
    backward = jnp.swapaxes(earlier[::-1], 0, 1).reshape(2, reach_shards * shard_len, head_size)
    padding = jnp.zeros((2, span, head_size), jnp.bfloat16)
    joined = jnp.concatenate([padding, backward, whole], axis=1)
    start = span + reach_shards * shard_len + sub_place * local_rows + local_rows - span
    window_rows = lax.dynamic_slice_in_dim(joined, start, span, 1)
    key_places = first_row + local_rows - span + jnp.arange(span, dtype=jnp.int32)
    piece = math.gcd(span, 512)
    pieces = span // piece
    stacked = jnp.swapaxes(window_rows.reshape(2, pieces, piece, head_size), 0, 1)
    place_pieces = key_places.reshape(pieces, piece)
    query_places = first_row + jnp.arange(local_rows, dtype=jnp.int32)
    highest, stored = masked_logits(
        queries, query_places, stacked, place_pieces, block_docs, windows, block_size
    )
    numerator, denominator = row_sums(queries, highest, stored, stacked[:, 1])
    return (numerator / denominator[:, :, None]).astype(jnp.bfloat16)


def solution(mesh):
    in_specs = (
        P(("ctx", "sub"), None, None),
        P(("ctx", "sub"), None),
        P(("ctx", "sub"), None),
        P(),
        P(),
    )
    out_specs = P(("ctx", "sub"), None, None)
    return jax.shard_map(local, mesh=mesh, in_specs=in_specs, out_specs=out_specs, check_vma=False)
```

profile of v0, /device:TPU:40, one launch (start us, length us, event | category | flops | bytes accessed | tf_op | source)
XLA Modules:
  0.0 353.4 jit_solution(12702805086697512239)
XLA Ops:
  8.0 106.6 %all-gather.2.cloned.1.call-done = bf16[2,6144,128]{2,1,0:T(8,128)(2,1)} async-done(((bf16[2,128,128]{2,1,0:T(8,128)(2,1)}), bf16[2,6144,128]{2,1,0:T(8,128)(2,1)}) %all-gather.2.cloned.1.call-update) | async-done | bytes 3145744 | tf_op jit(solution)/shard_map/all_gather | solution.py:84
  114.6 3.4 collective-permute-start
  119.1 139.5 %collective-permute-done = bf16[2,6144,128]{2,1,0:T(8,128)(2,1)} collective-permute-done((bf16[2,6144,128]{2,1,0:T(8,128)(2,1)}, bf16[2,6144,128]{2,1,0:T(8,128)(2,1)}, u32[]{:S(2)}, u32[]{:S(2)}) %collective-permute-start) | collective-permute-done | bytes 3145760 | tf_op jit(solution)/shard_map/while/body/eval_jaxpr/ppermute | solution.py:15
  258.7 2.5 fusion.18
  262.3 25.8 %while.37 = (s32[]{:T(128)}, f32[128,8]{0,1:T(8,128)S(1)}, f32[8,128,8,512]{1,3,2,0:T(8,128)}, s32[768]{0:T(1024)S(1)}, s32[8,512]{1,0:T(8,128)S(1)}, /*index=5*...) while((s32[]{:T(128)}, f32[128,8]{0,1:T(8,128)S(1)}, ...), condition=%wide.region_4.5_spmd.clone.clone.clone, body=%wide.region_0.4_spmd.clone.clone.clone.sunk | while | flops 138659840 | bytes 7915139 | solution.py:50
  264.0 1.5 bitcast_dynamic-update-slice_fusion.2
  270.4 1.5 bitcast_dynamic-update-slice_fusion.2
  273.6 1.5 bitcast_dynamic-update-slice_fusion.2
  276.8 1.6 bitcast_dynamic-update-slice_fusion.2
  283.3 1.5 bitcast_dynamic-update-slice_fusion.2
  286.5 1.5 bitcast_dynamic-update-slice_fusion.2
  288.0 57.4 %while.36 = (s32[]{:T(128)}, f32[128,8,128]{2,0,1:T(8,128)S(1)}, f32[128,8]{0,1:T(8,128)S(1)}, f32[8,128,8,512]{1,3,2,0:T(8,128)}, f32[128,8]{0,1:T(8,128)S(1)},...) while((s32[]{:T(128)}, f32[128,8,128]{2,0,1:T(8,128)S(1)}, f32[128,8]{0,1:T(8,128)S(1)}, ...), condition=%wide.region_7.8_spmd.clone, body=%wide.region_5.7_spmd.clone.sunk | while | flops 137626624 | bytes 13787748 | solution.py:68
  288.0 3.1 constant_dynamic-slice_fusion.4
  291.1 1.9 copy.26
  295.2 3.1 constant_dynamic-slice_fusion.4
  298.3 1.9 copy.26
  300.2 1.5 convolution_add_fusion.2
  302.4 3.1 constant_dynamic-slice_fusion.4
  305.5 1.9 copy.26
  307.4 1.5 convolution_add_fusion.2
  309.5 3.1 constant_dynamic-slice_fusion.4
  312.6 1.9 copy.26
  314.6 1.5 convolution_add_fusion.2
  316.7 3.1 constant_dynamic-slice_fusion.4
  319.8 1.9 copy.26
  323.9 3.1 constant_dynamic-slice_fusion.4
  327.0 1.9 copy.26
  331.1 3.1 constant_dynamic-slice_fusion.4
  334.2 1.9 copy.26
  338.2 3.1 constant_dynamic-slice_fusion.4
  341.3 1.9 copy.26
  343.3 1.5 convolution_add_fusion.2
  (128 shorter events, 32.1 us)
Async XLA Ops:
  6.5 108.0 %all-gather.2.cloned.1.call-start = ((), (), s32[]{:S(2)}) async-start(), calls=%async_computation | async-start | bytes 3211264 | tf_op jit(solution)/shard_map/all_gather | solution.py:84
  114.6 144.1 %collective-permute-start = (bf16[2,6144,128]{2,1,0:T(8,128)(2,1)}, bf16[2,6144,128]{2,1,0:T(8,128)(2,1)}, u32[]{:S(2)}, u32[]{:S(2)}) collective-permute-start(bf16[2,6144,128]{2,1,0:T(8,128)(2,1)} %all-gather.2.cloned.1.call-done), channel_id=1, source_target_pairs={{0,48},{48,96},{96,144},{144,192},{192,240},{240,288},{288,336},{3... | collective-permute-start | bytes 9437192 | tf_op jit(solution)/shard_map/while/body/eval_jaxpr/ppermute | solution.py:15
  261.2 1.1 copy-start
  261.2 1.1 copy-start.1
Sparse Core Ops, SparseCore 0:
  9.8 104.7 all-gather.1
where the time goes:
time: 354 us; the launch traced here: 353 us
  waiting for transfers between devices  246 us (69%)
  local copies, waits for them, and re-layouts  54.6 us (15%)
  other arithmetic  18.2 us (5%)
  matrix products  16.9 us (5%)
  between operations  13.5 us (4%)
    ppermute x1, waiting for transfers between devices, from_behind(): lax.ppermute(value, axis, [(source, source + steps) for source in range(i...  140 us
    all_gather x1, waiting for transfers between devices, local(): whole = lax.all_gather(paired, 'sub', axis=1, tiled=True)  107 us
    dynamic_slice x16, local copies, waits for them, and re-layouts, row_sums(): totals, unused = lax.scan(row_visit_piece, initial, (stored, value_pieces))  40.1 us
    dynamic_update_slice x8, local copies, waits for them, and re-layouts, masked_logits(): return lax.scan(masked_visit_piece, initial, (stacked, key_places))  12 us
    dot_general x8, matrix products, row_visit_piece(): jnp.einsum('qhk,kd->qhd', weights, values, preferred_element_type=jnp.flo...  11.8 us
  transfers between devices with their start and end apart: 2, of which 2 were waited for; matrix products, arithmetic and copies ran while one was open for 0% of the time, Pallas kernels for 0%

commit v1 on v0

v1 whole, which is shorter than its diff:
```python
import functools

import jax
import jax.numpy as jnp
from jax import lax
from jax.experimental import pallas as pl
from jax.experimental.pallas import tpu as pltpu
from jax.sharding import PartitionSpec as P

BLK = 128
WMAX = 32
LEVEL = 4
DEPTH = (WMAX - 1 + LEVEL - 1) // LEVEL + 1
MESH = pl.DeviceIdType.MESH


def relay_kernel(n_ctx, n_sub, kv_ref, got_ref, recv_sem, relay_sem, sib_sem, cross_sem, fwd_sem, own_sem):
    c = lax.axis_index("ctx")
    s = lax.axis_index("sub")
    total = n_ctx * n_sub
    g = c * n_sub + s
    q = s % LEVEL
    succ_g = (g + LEVEL) % total
    pred_g = (g + total - LEVEL) % total
    succ = (succ_g // n_sub, succ_g % n_sub)
    pred = (pred_g // n_sub, pred_g % n_sub)
    sib_q = q + 1 - 2 * (q % 2)
    cross_q = q + 2 - 4 * ((q // 2) % 2)
    sib = (c, s - q + sib_q)
    cross = (c, s - q + cross_q)

    barrier = pltpu.get_barrier_semaphore()
    for peer in (succ, pred, sib, cross):
        pl.semaphore_signal(barrier, inc=1, device_id=peer, device_id_type=MESH)
    pl.semaphore_wait(barrier, 4)

    own = pltpu.make_async_copy(kv_ref, got_ref.at[0, q], own_sem.at[0])
    own.start()

    def remote(src, k, col, peer, sem):
        return pltpu.make_async_remote_copy(
            src_ref=src,
            dst_ref=got_ref.at[k, col],
            send_sem=sem,
            recv_sem=recv_sem.at[k, col],
            device_id=peer,
            device_id_type=MESH,
        )

    sends = []
    for k in range(DEPTH):
        src = kv_ref if k == 0 else got_ref.at[k, q]
        if k > 0:
            remote(src, k, q, pred, relay_sem.at[k - 1]).wait_recv()
        if k + 1 < DEPTH:
            cp = remote(src, k + 1, q, succ, relay_sem.at[k])
            cp.start()
            sends.append(cp)
        cp = remote(src, k, q, sib, sib_sem.at[k])
        cp.start()
        sends.append(cp)
        cp = remote(src, k, q, cross, cross_sem.at[k])
        cp.start()
        sends.append(cp)
        got_cross = got_ref.at[k, cross_q]
        remote(got_cross, k, cross_q, cross, cross_sem.at[k]).wait_recv()
        cp = remote(got_cross, k, cross_q, sib, fwd_sem.at[k])
        cp.start()
        sends.append(cp)

    far_q = 3 - q
    for k in range(DEPTH):
        remote(got_ref.at[k, sib_q], k, sib_q, sib, sib_sem.at[k]).wait_recv()
        remote(got_ref.at[k, far_q], k, far_q, sib, fwd_sem.at[k]).wait_recv()
    for cp in sends:
        cp.wait_send()
    own.wait()


def relay(kv, n_ctx, n_sub):
    return pl.pallas_call(
        functools.partial(relay_kernel, n_ctx, n_sub),
        out_shape=jax.ShapeDtypeStruct((DEPTH, LEVEL) + kv.shape, kv.dtype),
        in_specs=[pl.BlockSpec(memory_space=pltpu.VMEM)],
        out_specs=pl.BlockSpec(memory_space=pl.ANY),
        scratch_shapes=[
            pltpu.SemaphoreType.DMA((DEPTH, LEVEL)),
            pltpu.SemaphoreType.DMA((DEPTH,)),
            pltpu.SemaphoreType.DMA((DEPTH,)),
            pltpu.SemaphoreType.DMA((DEPTH,)),
            pltpu.SemaphoreType.DMA((DEPTH,)),
            pltpu.SemaphoreType.DMA((1,)),
        ],
        compiler_params=pltpu.CompilerParams(collective_id=0, has_side_effects=True),
    )(kv)


def attend_kernel(ok_ref, dist_ref, q_ref, got_ref, win_ref, out_ref, s_sc, m_sc, num_sc, den_sc):
    rows, hd = q_ref.shape
    chunk = s_sc.shape[1]
    slots = s_sc.shape[0]
    heads = rows // BLK
    scale = hd ** -0.5

    def one_chunk(ci, carry):
        r0 = pl.multiple_of(ci * chunk, chunk)
        qc = q_ref[pl.ds(r0, chunk), :]
        win = win_ref[pl.ds(r0, chunk), :]
        query_i = (lax.broadcasted_iota(jnp.int32, (chunk, BLK), 0) + r0) // heads
        key_j = lax.broadcasted_iota(jnp.int32, (chunk, BLK), 1)
        m_sc[...] = jnp.full(m_sc.shape, -jnp.inf, jnp.float32)
        num_sc[...] = jnp.zeros(num_sc.shape, jnp.float32)
        den_sc[...] = jnp.zeros(den_sc.shape, jnp.float32)

        def first(slot, c2):
            d = dist_ref[slot]

            @pl.when(ok_ref[slot] != 0)
            def _():
                kb = got_ref[slot // LEVEL, slot % LEVEL, 0]
                sc = lax.dot_general(qc, kb, (((1,), (1,)), ((), ())), preferred_element_type=jnp.float32) * scale
                allowed = (d < win) & ((d > 0) | (key_j <= query_i))
                sc = jnp.where(allowed, sc, -jnp.inf)
                s_sc[slot] = sc
                m_sc[...] = jnp.maximum(m_sc[...], jnp.max(sc, axis=1, keepdims=True))

            return c2

        lax.fori_loop(0, slots, first, 0)

        def second(slot, c2):
            @pl.when(ok_ref[slot] != 0)
            def _():
                w = jnp.exp(s_sc[slot] - m_sc[...]).astype(jnp.bfloat16)
                vb = got_ref[slot // LEVEL, slot % LEVEL, 1]
                num_sc[...] += jnp.dot(w, vb, preferred_element_type=jnp.float32)
                den_sc[...] += jnp.sum(w.astype(jnp.float32), axis=1, keepdims=True)

            return c2

        lax.fori_loop(0, slots, second, 0)
        out_ref[pl.ds(r0, chunk), :] = (num_sc[...] / den_sc[...]).astype(out_ref.dtype)
        return carry

    lax.fori_loop(0, rows // chunk, one_chunk, 0)


def attend(ok, dist, q2, got, win_rows):
    rows, hd = q2.shape
    chunk = 256
    slots = DEPTH * LEVEL
    return pl.pallas_call(
        attend_kernel,
        out_shape=jax.ShapeDtypeStruct((rows, hd), q2.dtype),
        in_specs=[
            pl.BlockSpec(memory_space=pltpu.SMEM),
            pl.BlockSpec(memory_space=pltpu.SMEM),
            pl.BlockSpec(memory_space=pltpu.VMEM),
            pl.BlockSpec(memory_space=pltpu.VMEM),
            pl.BlockSpec(memory_space=pltpu.VMEM),
        ],
        out_specs=pl.BlockSpec(memory_space=pltpu.VMEM),
        scratch_shapes=[
            pltpu.VMEM((slots, chunk, BLK), jnp.float32),
            pltpu.VMEM((chunk, 1), jnp.float32),
            pltpu.VMEM((chunk, hd), jnp.float32),
            pltpu.VMEM((chunk, 1), jnp.float32),
        ],
        compiler_params=pltpu.CompilerParams(vmem_limit_bytes=48 * 1024 * 1024),
    )(ok, dist, q2, got, win_rows)


def local(queries, key_rows, value_rows, block_docs, windows):
    n_ctx = lax.axis_size("ctx")
    n_sub = lax.axis_size("sub")
    c = lax.axis_index("ctx")
    s = lax.axis_index("sub")
    g = c * n_sub + s
    q = s % LEVEL
    rows_here, heads, hd = queries.shape
    kv = jnp.stack([key_rows, value_rows])
    got = relay(kv, n_ctx, n_sub)

    k_of = jnp.arange(DEPTH * LEVEL, dtype=jnp.int32) // LEVEL
    col_of = jnp.arange(DEPTH * LEVEL, dtype=jnp.int32) % LEVEL
    dist = LEVEL * k_of + q - col_of
    key_block = g - dist
    doc_here = block_docs[g]
    doc_there = jnp.take(block_docs, jnp.clip(key_block, 0, block_docs.shape[0] - 1))
    ok = (dist >= 0) & (dist < WMAX) & (key_block >= 0) & (doc_there == doc_here)
    win_rows = jnp.tile(windows, rows_here).reshape(rows_here * heads, 1)
    out = attend(ok.astype(jnp.int32), dist, queries.reshape(rows_here * heads, hd), got, win_rows)
    return out.reshape(rows_here, heads, hd)


def solution(mesh):
    in_specs = (
        P(("ctx", "sub"), None, None),
        P(("ctx", "sub"), None),
        P(("ctx", "sub"), None),
        P(),
        P(),
    )
    out_specs = P(("ctx", "sub"), None, None)
    return jax.shard_map(local, mesh=mesh, in_specs=in_specs, out_specs=out_specs, check_vma=False)
```

time: 354 us -> 142 us (0.40)
  the two profiles are of different devices: /device:TPU:40 before, /device:TPU:47 now
where the time goes in v1:
time: 142 us
  Pallas kernels  134 us (94%)
  local copies, waits for them, and re-layouts  5.28 us (4%)
  other arithmetic  2.1 us (1%)
    pallas_call x1, Pallas kernels, attend(): pl.pallas_call(attend_kernel, out_shape=jax.ShapeDtypeStruct((rows, hd),...  67.9 us
    pallas_call x1, Pallas kernels, relay(): pl.pallas_call(functools.partial(relay_kernel, n_ctx, n_sub), out_shape=j...  66.5 us

profile of v1, /device:TPU:47, one launch (start us, length us, event | category | flops | bytes accessed | tf_op | source)
XLA Modules:
  0.0 141.8 jit_solution(1396180057923128127)
XLA Ops:
  0.0 0.0 copy-start.1
  0.0 1.3 dynamic_slice.3
  1.4 1.5 %gather_fusion = s32[36]{0:T(128)S(1)} fusion(s32[768]{0:T(1024)} %param.8, s32[1024]{0:T(1024)S(1)} %pad_clamp_fusion), kind=kCustom, calls=%fused_computation | custom fusion | bytes 432 | tf_op jit(solution)/shard_map/jit(_take)/gather | solution.py:189
  2.8 0.7 and_convert_fusion.ok_ref
  3.5 1.4 pad_maximum_fusion.kv_ref
  4.9 0.7 tile.2
  5.6 0.2 reshape_tile.4.win_ref
  5.8 66.5 %shard_map.55.got_ref = bf16[9,4,2,128,128]{4,3,2,1,0:T(8,128)(2,1)} custom-call(bf16[2,128,128]{2,1,0:T(8,128)(2,1)} %pad_maximum_fusion.kv_ref), custom_call_target="tpu_custom_call" | custom-call | tf_op jit(solution)/shard_map/pallas_call | solution.py:81
  72.2 0.0 copy-done.1
  72.2 0.0 copy-start
  72.2 1.7 %copy-done = bf16[9,4,2,128,128]{4,3,2,1,0:T(8,128)(2,1)S(1)} copy-done((bf16[9,4,2,128,128]{4,3,2,1,0:T(8,128)(2,1)S(1)}, bf16[9,4,2,128,128]{4,3,2,1,0:T(8,128)(2,1)}, u32[]{:S(2)}) %copy-start) | copy-done | bytes 2359320
  73.9 67.9 %shard_map.56 = bf16[1024,128]{1,0:T(8,128)(2,1)} custom-call(s32[36]{0:T(128)S(1)} %and_convert_fusion.ok_ref, s32[36]{0:T(128)S(1)} %fusion.dist_ref, bf16[1024,128]{1,0:T(8,128)(2,1)S(1)} %bitcast.7, bf16[9,4,2,128,128]{4,3,2,1,0:T(8,128)(2,1)S(1)} %copy-done, s32[1024,1]{1,0:T(8,128)S(1)} %reshape_tile.4.win_ref), custom_call_target="tpu_custom_call" | custom-call | tf_op jit(solution)/shard_map/pallas_call | solution.py:152
  (3 shorter events, 0.0 us)
Async XLA Ops:
  0.0 72.2 %copy-start.1 = (bf16[128,8,128]{2,1,0:T(8,128)(2,1)S(1)}, bf16[128,8,128]{2,1,0:T(8,128)(2,1)}, u32[]{:S(2)}) copy-start(bf16[128,8,128]{2,1,0:T(8,128)(2,1)} %param.5) | copy-start | bytes 786436
  72.2 1.7 %copy-start = (bf16[9,4,2,128,128]{4,3,2,1,0:T(8,128)(2,1)S(1)}, bf16[9,4,2,128,128]{4,3,2,1,0:T(8,128)(2,1)}, u32[]{:S(2)}) copy-start(bf16[9,4,2,128,128]{4,3,2,1,0:T(8,128)(2,1)} %shard_map.55.got_ref) | copy-start | bytes 7077892

commit v2 on v1

--- a/solution.py
+++ b/solution.py
@@ -56,12 +56,14 @@
             cp = remote(src, k + 1, q, succ, relay_sem.at[k])
             cp.start()
             sends.append(cp)
+        cp = remote(src, k, q, cross, cross_sem.at[k])
+        cp.start()
+        sends.append(cp)
         cp = remote(src, k, q, sib, sib_sem.at[k])
         cp.start()
         sends.append(cp)
-        cp = remote(src, k, q, cross, cross_sem.at[k])
-        cp.start()
-        sends.append(cp)
+
+    for k in range(DEPTH):
         got_cross = got_ref.at[k, cross_q]
         remote(got_cross, k, cross_q, cross, cross_sem.at[k]).wait_recv()
         cp = remote(got_cross, k, cross_q, sib, fwd_sem.at[k])
@@ -105,9 +107,9 @@
     def one_chunk(ci, carry):
         r0 = pl.multiple_of(ci * chunk, chunk)
         qc = q_ref[pl.ds(r0, chunk), :]
-        win = win_ref[pl.ds(r0, chunk), :]
         query_i = (lax.broadcasted_iota(jnp.int32, (chunk, BLK), 0) + r0) // heads
         key_j = lax.broadcasted_iota(jnp.int32, (chunk, BLK), 1)
+        causal = key_j <= query_i
         m_sc[...] = jnp.full(m_sc.shape, -jnp.inf, jnp.float32)
         num_sc[...] = jnp.zeros(num_sc.shape, jnp.float32)
         den_sc[...] = jnp.zeros(den_sc.shape, jnp.float32)
@@ -119,27 +121,29 @@
             def _():
                 kb = got_ref[slot // LEVEL, slot % LEVEL, 0]
                 sc = lax.dot_general(qc, kb, (((1,), (1,)), ((), ())), preferred_element_type=jnp.float32) * scale
-                allowed = (d < win) & ((d > 0) | (key_j <= query_i))
+                allowed = (win_ref[pl.ds(r0, chunk), :] > d) & (causal | (d > 0))
                 sc = jnp.where(allowed, sc, -jnp.inf)
                 s_sc[slot] = sc
-                m_sc[...] = jnp.maximum(m_sc[...], jnp.max(sc, axis=1, keepdims=True))
+                m_sc[...] = jnp.maximum(m_sc[...], sc)
 
             return c2
 
         lax.fori_loop(0, slots, first, 0)
+        m = jnp.max(m_sc[...], axis=1, keepdims=True)
 
         def second(slot, c2):
             @pl.when(ok_ref[slot] != 0)
             def _():
-                w = jnp.exp(s_sc[slot] - m_sc[...]).astype(jnp.bfloat16)
+                w = jnp.exp(s_sc[slot] - m).astype(jnp.bfloat16)
                 vb = got_ref[slot // LEVEL, slot % LEVEL, 1]
                 num_sc[...] += jnp.dot(w, vb, preferred_element_type=jnp.float32)
-                den_sc[...] += jnp.sum(w.astype(jnp.float32), axis=1, keepdims=True)
+                den_sc[...] += w.astype(jnp.float32)
 
             return c2
 
         lax.fori_loop(0, slots, second, 0)
-        out_ref[pl.ds(r0, chunk), :] = (num_sc[...] / den_sc[...]).astype(out_ref.dtype)
+        den = jnp.sum(den_sc[...], axis=1, keepdims=True)
+        out_ref[pl.ds(r0, chunk), :] = (num_sc[...] / den).astype(out_ref.dtype)
         return carry
 
     lax.fori_loop(0, rows // chunk, one_chunk, 0)
@@ -147,7 +151,7 @@
 
 def attend(ok, dist, q2, got, win_rows):
     rows, hd = q2.shape
-    chunk = 256
+    chunk = 512
     slots = DEPTH * LEVEL
     return pl.pallas_call(
         attend_kernel,
@@ -162,9 +166,9 @@
         out_specs=pl.BlockSpec(memory_space=pltpu.VMEM),
         scratch_shapes=[
             pltpu.VMEM((slots, chunk, BLK), jnp.float32),
-            pltpu.VMEM((chunk, 1), jnp.float32),
+            pltpu.VMEM((chunk, BLK), jnp.float32),
             pltpu.VMEM((chunk, hd), jnp.float32),
-            pltpu.VMEM((chunk, 1), jnp.float32),
+            pltpu.VMEM((chunk, BLK), jnp.float32),
         ],
         compiler_params=pltpu.CompilerParams(vmem_limit_bytes=48 * 1024 * 1024),
     )(ok, dist, q2, got, win_rows)
@@ -188,7 +192,7 @@
     doc_here = block_docs[g]
     doc_there = jnp.take(block_docs, jnp.clip(key_block, 0, block_docs.shape[0] - 1))
     ok = (dist >= 0) & (dist < WMAX) & (key_block >= 0) & (doc_there == doc_here)
-    win_rows = jnp.tile(windows, rows_here).reshape(rows_here * heads, 1)
+    win_rows = jnp.broadcast_to(jnp.tile(windows, rows_here)[:, None], (rows_here * heads, BLK))
     out = attend(ok.astype(jnp.int32), dist, queries.reshape(rows_here * heads, hd), got, win_rows)
     return out.reshape(rows_here, heads, hd)
 

time: 142 us -> 91 us (0.64)
  the two profiles are of different devices: /device:TPU:47 before, /device:TPU:63 now
where the time goes in v2:
time: 91 us; the launch traced here: 90.7 us
  Pallas kernels  83.1 us (91%)
  local copies, waits for them, and re-layouts  5.38 us (6%)
  other arithmetic  2.1 us (2%)
    pallas_call x1, Pallas kernels, relay(): pl.pallas_call(functools.partial(relay_kernel, n_ctx, n_sub), out_shape=j...  53.9 us
    pallas_call x1, Pallas kernels, attend(): pl.pallas_call(attend_kernel, out_shape=jax.ShapeDtypeStruct((rows, hd),...  29.2 us

profile of v2, /device:TPU:63, one launch (start us, length us, event | category | flops | bytes accessed | tf_op | source)
XLA Modules:
  0.0 90.7 jit_solution(1256319452600291565)
XLA Ops:
  0.0 0.0 copy-start.1
  0.0 1.3 %dynamic_slice.3 = s32[1]{0:T(128)} dynamic-slice(s32[768]{0:T(1024)} %param.8, s32[]{:T(128)S(6)} %select_n.70), dynamic_slice_sizes={1} | dynamic-slice | bytes 12 | tf_op jit(solution)/shard_map/dynamic_slice | solution.py:192
  1.4 1.5 %gather_fusion = s32[36]{0:T(128)S(1)} fusion(s32[768]{0:T(1024)} %param.8, s32[1024]{0:T(1024)S(1)} %pad_clamp_fusion), kind=kCustom, calls=%fused_computation | custom fusion | bytes 432 | tf_op jit(solution)/shard_map/jit(_take)/gather | solution.py:193
  2.8 0.7 and_convert_fusion.ok_ref
  3.5 1.4 %pad_maximum_fusion.kv_ref = bf16[2,128,128]{2,1,0:T(8,128)(2,1)} fusion(bf16[1,128,128]{2,1,0:T(8,128)(2,1)} %bitcast.8, bf16[1,128,128]{2,1,0:T(8,128)(2,1)} %bitcast.9), kind=kLoop, calls=%fused_computation.1 | loop fusion | flops 32768 | bytes 131072 | tf_op jit(solution)/shard_map/stack | solution.py:185
  4.9 0.7 tile.2
  5.6 0.1 broadcast_in_dim.14
  5.7 0.2 broadcast_in_dim.15.win_ref
  5.9 53.9 %shard_map.55.got_ref = bf16[9,4,2,128,128]{4,3,2,1,0:T(8,128)(2,1)} custom-call(bf16[2,128,128]{2,1,0:T(8,128)(2,1)} %pad_maximum_fusion.kv_ref), custom_call_target="tpu_custom_call" | custom-call | tf_op jit(solution)/shard_map/pallas_call | solution.py:83
  59.8 0.0 copy-done.1
  59.8 0.0 copy-start
  59.8 1.7 %copy-done = bf16[9,4,2,128,128]{4,3,2,1,0:T(8,128)(2,1)S(1)} copy-done((bf16[9,4,2,128,128]{4,3,2,1,0:T(8,128)(2,1)S(1)}, bf16[9,4,2,128,128]{4,3,2,1,0:T(8,128)(2,1)}, u32[]{:S(2)}) %copy-start) | copy-done | bytes 2359320
  61.5 29.2 %shard_map.56 = bf16[1024,128]{1,0:T(8,128)(2,1)} custom-call(s32[36]{0:T(128)S(1)} %and_convert_fusion.ok_ref, s32[36]{0:T(128)S(1)} %fusion.dist_ref, bf16[1024,128]{1,0:T(8,128)(2,1)S(1)} %bitcast.7, bf16[9,4,2,128,128]{4,3,2,1,0:T(8,128)(2,1)S(1)} %copy-done, s32[1024,128]{1,0:T(8,128)S(1)} %broadcast_in_dim.15.win_ref), custom_call_target="tpu_custom_call" | custom-call | tf_op jit(solution)/shard_map/pallas_call | solution.py:156
  (3 shorter events, 0.0 us)
Async XLA Ops:
  0.0 59.8 %copy-start.1 = (bf16[128,8,128]{2,1,0:T(8,128)(2,1)S(1)}, bf16[128,8,128]{2,1,0:T(8,128)(2,1)}, u32[]{:S(2)}) copy-start(bf16[128,8,128]{2,1,0:T(8,128)(2,1)} %param.5) | copy-start | bytes 786436
  59.8 1.7 %copy-start = (bf16[9,4,2,128,128]{4,3,2,1,0:T(8,128)(2,1)S(1)}, bf16[9,4,2,128,128]{4,3,2,1,0:T(8,128)(2,1)}, u32[]{:S(2)}) copy-start(bf16[9,4,2,128,128]{4,3,2,1,0:T(8,128)(2,1)} %shard_map.55.got_ref) | copy-start | bytes 7077892

commit v3 on v1

v3 whole, which is shorter than its diff:
```python
import functools

import jax
import jax.numpy as jnp
from jax import lax
from jax.experimental import pallas as pl
from jax.experimental.pallas import tpu as pltpu
from jax.sharding import PartitionSpec as P

BLK = 128
WMAX = 32
LEVEL = 4
DEPTH = (WMAX - 1 + LEVEL - 1) // LEVEL + 1
MESH = pl.DeviceIdType.MESH
CHUNK = 256


def fused_kernel(n_ctx, n_sub, ok_ref, kv_ref, q_ref, win_ref, out_ref,
                 got, s_sc, m_sc, num_sc, den_sc,
                 recv_sem, relay_sem, sib_sem, cross_sem, fwd_sem, own_sem):
    c = lax.axis_index("ctx")
    s = lax.axis_index("sub")
    total = n_ctx * n_sub
    g = c * n_sub + s
    q = s % LEVEL
    succ_g = (g + LEVEL) % total
    pred_g = (g + total - LEVEL) % total
    succ = (succ_g // n_sub, succ_g % n_sub)
    pred = (pred_g // n_sub, pred_g % n_sub)
    sib_q = q + 1 - 2 * (q % 2)
    cross_q = q + 2 - 4 * ((q // 2) % 2)
    far_q = 3 - q
    sib = (c, s - q + sib_q)
    cross = (c, s - q + cross_q)
    rows, hd = q_ref.shape
    heads = rows // BLK
    scale = hd ** -0.5
    n_chunks = rows // CHUNK

    barrier = pltpu.get_barrier_semaphore()
    for peer in (succ, pred, sib, cross):
        pl.semaphore_signal(barrier, inc=1, device_id=peer, device_id_type=MESH)
    pl.semaphore_wait(barrier, 4)

    own = pltpu.make_async_copy(kv_ref, got.at[0, q], own_sem.at[0])
    own.start()

    def remote(src, k, col, peer, sem):
        return pltpu.make_async_remote_copy(
            src_ref=src,
            dst_ref=got.at[k, col],
            send_sem=sem,
            recv_sem=recv_sem.at[k, col],
            device_id=peer,
            device_id_type=MESH,
        )

    m_sc[...] = jnp.full(m_sc.shape, -jnp.inf, jnp.float32)

    def logits(k, col):
        slot = k * LEVEL + col
        d = LEVEL * k + q - col
        live = ok_ref[slot] != 0

        def body(ci, carry):
            r0 = pl.multiple_of(ci * CHUNK, CHUNK)
            qc = q_ref[pl.ds(r0, CHUNK), :]
            kb = got[k, col, 0]
            sc = lax.dot_general(qc, kb, (((1,), (1,)), ((), ())), preferred_element_type=jnp.float32) * scale
            query_i = (lax.broadcasted_iota(jnp.int32, (CHUNK, BLK), 0) + r0) // heads
            key_j = lax.broadcasted_iota(jnp.int32, (CHUNK, BLK), 1)
            allowed = (win_ref[pl.ds(r0, CHUNK), :] > d) & ((key_j <= query_i) | (d > 0)) & live
            sc = jnp.where(allowed, sc, -jnp.inf)
            s_sc[slot, pl.ds(r0, CHUNK), :] = sc
            m_sc[pl.ds(r0, CHUNK), :] = jnp.maximum(m_sc[pl.ds(r0, CHUNK), :], sc)
            return carry

        lax.fori_loop(0, n_chunks, body, 0)

    remote(kv_ref, 1, q, succ, relay_sem.at[0]).start()
    remote(kv_ref, 0, q, cross, cross_sem.at[0]).start()
    remote(kv_ref, 0, q, sib, sib_sem.at[0]).start()
    own.wait()
    logits(0, q)

    def relay_step(k, carry):
        src = got.at[k, q]
        remote(src, k, q, pred, relay_sem.at[k - 1]).wait_recv()

        @pl.when(k + 1 < DEPTH)
        def _():
            remote(src, k + 1, q, succ, relay_sem.at[k]).start()

        remote(src, k, q, cross, cross_sem.at[k]).start()
        remote(src, k, q, sib, sib_sem.at[k]).start()
        logits(k, q)
        return carry

    lax.fori_loop(1, DEPTH, relay_step, 0)

    def cross_step(k, carry):
        src = got.at[k, cross_q]
        remote(src, k, cross_q, cross, cross_sem.at[k]).wait_recv()
        remote(src, k, cross_q, sib, fwd_sem.at[k]).start()
        logits(k, cross_q)
        return carry

    lax.fori_loop(0, DEPTH, cross_step, 0)

    def sib_step(k, carry):
        remote(got.at[k, sib_q], k, sib_q, sib, sib_sem.at[k]).wait_recv()
        logits(k, sib_q)
        remote(got.at[k, far_q], k, far_q, sib, fwd_sem.at[k]).wait_recv()
        logits(k, far_q)
        return carry

    lax.fori_loop(0, DEPTH, sib_step, 0)

    num_sc[...] = jnp.zeros(num_sc.shape, jnp.float32)
    den_sc[...] = jnp.zeros(den_sc.shape, jnp.float32)

    def weigh_chunk(ci, carry):
        r0 = pl.multiple_of(ci * CHUNK, CHUNK)
        m = jnp.max(m_sc[pl.ds(r0, CHUNK), :], axis=1, keepdims=True)

        def weigh(slot, c2):
            w = jnp.exp(s_sc[slot, pl.ds(r0, CHUNK), :] - m).astype(jnp.bfloat16)
            vb = got[slot // LEVEL, slot % LEVEL, 1]
            num_sc[pl.ds(r0, CHUNK), :] += jnp.dot(w, vb, preferred_element_type=jnp.float32)
            den_sc[pl.ds(r0, CHUNK), :] += w.astype(jnp.float32)
            return c2

        lax.fori_loop(0, DEPTH * LEVEL, weigh, 0)
        den = jnp.sum(den_sc[pl.ds(r0, CHUNK), :], axis=1, keepdims=True)
        out_ref[pl.ds(r0, CHUNK), :] = (num_sc[pl.ds(r0, CHUNK), :] / den).astype(out_ref.dtype)
        return carry

    lax.fori_loop(0, n_chunks, weigh_chunk, 0)

    def drain(k, carry):
        @pl.when(k + 1 < DEPTH)
        def _():
            remote(got.at[k, q], k + 1, q, succ, relay_sem.at[k]).wait_send()

        remote(got.at[k, q], k, q, cross, cross_sem.at[k]).wait_send()
        remote(got.at[k, q], k, q, sib, sib_sem.at[k]).wait_send()
        remote(got.at[k, cross_q], k, cross_q, sib, fwd_sem.at[k]).wait_send()
        return carry

    lax.fori_loop(0, DEPTH, drain, 0)


def fused(ok, kv, q2, win_rows, n_ctx, n_sub):
    rows, hd = q2.shape
    slots = DEPTH * LEVEL
    return pl.pallas_call(
        functools.partial(fused_kernel, n_ctx, n_sub),
        out_shape=jax.ShapeDtypeStruct((rows, hd), q2.dtype),
        in_specs=[
            pl.BlockSpec(memory_space=pltpu.SMEM),
            pl.BlockSpec(memory_space=pltpu.VMEM),
            pl.BlockSpec(memory_space=pltpu.VMEM),
            pl.BlockSpec(memory_space=pltpu.VMEM),
        ],
        out_specs=pl.BlockSpec(memory_space=pltpu.VMEM),
        scratch_shapes=[
            pltpu.VMEM((DEPTH, LEVEL) + kv.shape, kv.dtype),
            pltpu.VMEM((slots, rows, BLK), jnp.float32),
            pltpu.VMEM((rows, BLK), jnp.float32),
            pltpu.VMEM((rows, hd), jnp.float32),
            pltpu.VMEM((rows, BLK), jnp.float32),
            pltpu.SemaphoreType.DMA((DEPTH, LEVEL)),
            pltpu.SemaphoreType.DMA((DEPTH,)),
            pltpu.SemaphoreType.DMA((DEPTH,)),
            pltpu.SemaphoreType.DMA((DEPTH,)),
            pltpu.SemaphoreType.DMA((DEPTH,)),
            pltpu.SemaphoreType.DMA((1,)),
        ],
        compiler_params=pltpu.CompilerParams(
            collective_id=0, has_side_effects=True, vmem_limit_bytes=60 * 1024 * 1024
        ),
    )(ok, kv, q2, win_rows)


def local(queries, key_rows, value_rows, block_docs, windows):
    n_ctx = lax.axis_size("ctx")
    n_sub = lax.axis_size("sub")
    c = lax.axis_index("ctx")
    s = lax.axis_index("sub")
    g = c * n_sub + s
    q = s % LEVEL
    rows_here, heads, hd = queries.shape
    kv = jnp.stack([key_rows, value_rows])

    k_of = jnp.arange(DEPTH * LEVEL, dtype=jnp.int32) // LEVEL
    col_of = jnp.arange(DEPTH * LEVEL, dtype=jnp.int32) % LEVEL
    dist = LEVEL * k_of + q - col_of
    key_block = g - dist
    doc_here = block_docs[g]
    doc_there = jnp.take(block_docs, jnp.clip(key_block, 0, block_docs.shape[0] - 1))
    ok = (dist >= 0) & (dist < WMAX) & (key_block >= 0) & (doc_there == doc_here)
    win_rows = jnp.broadcast_to(jnp.tile(windows, rows_here)[:, None], (rows_here * heads, BLK))
    out = fused(ok.astype(jnp.int32), kv, queries.reshape(rows_here * heads, hd), win_rows, n_ctx, n_sub)
    return out.reshape(rows_here, heads, hd)


def solution(mesh):
    in_specs = (
        P(("ctx", "sub"), None, None),
        P(("ctx", "sub"), None),
        P(("ctx", "sub"), None),
        P(),
        P(),
    )
    out_specs = P(("ctx", "sub"), None, None)
    return jax.shard_map(local, mesh=mesh, in_specs=in_specs, out_specs=out_specs, check_vma=False)
```

time: 142 us -> 101 us (0.71)
  the two profiles are of different devices: /device:TPU:47 before, /device:TPU:128 now
where the time goes in v3:
time: 101 us
  Pallas kernels  94 us (93%)
  local copies, waits for them, and re-layouts  4.79 us (5%)
  other arithmetic  1.86 us (2%)
    pallas_call x1, Pallas kernels, fused(): pl.pallas_call(functools.partial(fused_kernel, n_ctx, n_sub), out_shape=j...  94 us
    unnamed x9, local copies, waits for them, and re-layouts  2.39 us

profile of v3, /device:TPU:128, one launch (start us, length us, event | category | flops | bytes accessed | tf_op | source)
XLA Modules:
  0.0 100.7 jit_solution(18338800193311971417)
XLA Ops:
  0.0 0.0 copy-start
  0.0 0.7 copy-done
  0.7 0.6 dynamic_slice.3
  1.3 0.0 copy-start.1
  1.3 0.0 copy-start.2
  1.3 0.7 gather_fusion
  2.1 1.2 %and_convert_fusion.ok_ref = s32[36]{0:T(128)} fusion(s32[36]{0:T(128)S(1)} %gather_fusion, s32[]{:T(128)} %bitcast.1, s32[]{:T(128)S(6)} %add.81, s32[]{:T(128)S(6)} %select_n.63), kind=kLoop, calls=%fused_computation.5 | loop fusion | flops 1152 | bytes 300 | tf_op jit(solution)/shard_map/convert_element_type | solution.py:203
  3.3 0.0 copy-done.1
  3.3 0.0 copy-done.2
  3.3 0.0 copy-start.3
  3.3 0.6 pad_maximum_fusion.kv_ref
  3.9 0.0 copy-done.3
  3.9 0.1 broadcast_in_dim.14
  4.0 1.0 broadcast_in_dim.15.win_ref
  5.0 94.0 %shard_map.55 = bf16[1024,128]{1,0:T(8,128)(2,1)} custom-call(s32[36]{0:T(128)} %and_convert_fusion.ok_ref, bf16[2,128,128]{2,1,0:T(8,128)(2,1)} %pad_maximum_fusion.kv_ref, bf16[1024,128]{1,0:T(8,128)(2,1)} %bitcast.8, s32[1024,128]{1,0:T(8,128)} %broadcast_in_dim.15.win_ref), custom_call_target="tpu_custom_call" | custom-call | tf_op jit(solution)/shard_map/pallas_call | solution.py:156
  99.0 1.7 %copy.7 = bf16[128,8,128]{2,1,0:T(8,128)(2,1)} copy(bf16[128,8,128]{2,1,0:T(8,128)(2,1)} %bitcast.7) | data formatting | bytes 524288
  (3 shorter events, 0.0 us)
Async XLA Ops:
  0.0 0.7 copy-start
  1.3 2.0 %copy-start.1 = (bf16[128,128]{1,0:T(8,128)(2,1)S(1)}, bf16[128,128]{1,0:T(8,128)(2,1)}, u32[]{:S(2)}) copy-start(bf16[128,128]{1,0:T(8,128)(2,1)} %param.7) | copy-start | bytes 98308
  1.3 1.9 %copy-start.2 = (bf16[128,128]{1,0:T(8,128)(2,1)S(1)}, bf16[128,128]{1,0:T(8,128)(2,1)}, u32[]{:S(2)}) copy-start(bf16[128,128]{1,0:T(8,128)(2,1)} %param.6) | copy-start | bytes 98308
  3.3 0.7 copy-start.3

commit v4 on v3

--- a/solution.py
+++ b/solution.py
@@ -56,32 +56,38 @@
         )
 
     m_sc[...] = jnp.full(m_sc.shape, -jnp.inf, jnp.float32)
-
-    def logits(k, col):
+    win8 = win_ref[...]
+
+    def logits(k, col, causal=False):
         slot = k * LEVEL + col
         d = LEVEL * k + q - col
         live = ok_ref[slot] != 0
 
-        def body(ci, carry):
-            r0 = pl.multiple_of(ci * CHUNK, CHUNK)
-            qc = q_ref[pl.ds(r0, CHUNK), :]
-            kb = got[k, col, 0]
-            sc = lax.dot_general(qc, kb, (((1,), (1,)), ((), ())), preferred_element_type=jnp.float32) * scale
-            query_i = (lax.broadcasted_iota(jnp.int32, (CHUNK, BLK), 0) + r0) // heads
-            key_j = lax.broadcasted_iota(jnp.int32, (CHUNK, BLK), 1)
-            allowed = (win_ref[pl.ds(r0, CHUNK), :] > d) & ((key_j <= query_i) | (d > 0)) & live
-            sc = jnp.where(allowed, sc, -jnp.inf)
-            s_sc[slot, pl.ds(r0, CHUNK), :] = sc
-            m_sc[pl.ds(r0, CHUNK), :] = jnp.maximum(m_sc[pl.ds(r0, CHUNK), :], sc)
-            return carry
-
-        lax.fori_loop(0, n_chunks, body, 0)
+        @pl.when((d >= 0) & (d < WMAX) & (g >= d))
+        def _():
+            allowed = (win8 > d) & live
+
+            def body(ci, carry):
+                r0 = pl.multiple_of(ci * CHUNK, CHUNK)
+                qc = q_ref[pl.ds(r0, CHUNK), :]
+                kb = got[k, col, 0]
+                sc = lax.dot_general(qc, kb, (((1,), (1,)), ((), ())), preferred_element_type=jnp.float32) * scale
+                sc = sc.reshape(CHUNK // heads, heads, BLK)
+                keep = allowed[None]
+                if causal:
+                    query_i = lax.broadcasted_iota(jnp.int32, sc.shape, 0) + r0 // heads
+                    key_j = lax.broadcasted_iota(jnp.int32, sc.shape, 2)
+                    keep = keep & (key_j <= query_i)
+                sc = jnp.where(keep, sc, -jnp.inf).reshape(CHUNK, BLK)
+                s_sc[slot, pl.ds(r0, CHUNK), :] = sc
+                m_sc[pl.ds(r0, CHUNK), :] = jnp.maximum(m_sc[pl.ds(r0, CHUNK), :], sc)
+                return carry
+
+            lax.fori_loop(0, n_chunks, body, 0)
 
     remote(kv_ref, 1, q, succ, relay_sem.at[0]).start()
     remote(kv_ref, 0, q, cross, cross_sem.at[0]).start()
     remote(kv_ref, 0, q, sib, sib_sem.at[0]).start()
-    own.wait()
-    logits(0, q)
 
     def relay_step(k, carry):
         src = got.at[k, q]
@@ -93,7 +99,6 @@
 
         remote(src, k, q, cross, cross_sem.at[k]).start()
         remote(src, k, q, sib, sib_sem.at[k]).start()
-        logits(k, q)
         return carry
 
     lax.fori_loop(1, DEPTH, relay_step, 0)
@@ -102,10 +107,20 @@
         src = got.at[k, cross_q]
         remote(src, k, cross_q, cross, cross_sem.at[k]).wait_recv()
         remote(src, k, cross_q, sib, fwd_sem.at[k]).start()
+        return carry
+
+    lax.fori_loop(0, DEPTH, cross_step, 0)
+
+    own.wait()
+    logits(0, q, causal=True)
+
+    def here_step(k, carry):
+        logits(k, q)
         logits(k, cross_q)
         return carry
 
-    lax.fori_loop(0, DEPTH, cross_step, 0)
+    lax.fori_loop(1, DEPTH, here_step, 0)
+    logits(0, cross_q)
 
     def sib_step(k, carry):
         remote(got.at[k, sib_q], k, sib_q, sib, sib_sem.at[k]).wait_recv()
@@ -121,13 +136,20 @@
 
     def weigh_chunk(ci, carry):
         r0 = pl.multiple_of(ci * CHUNK, CHUNK)
-        m = jnp.max(m_sc[pl.ds(r0, CHUNK), :], axis=1, keepdims=True)
+        m_sc[pl.ds(r0, CHUNK), :] = jnp.broadcast_to(
+            jnp.max(m_sc[pl.ds(r0, CHUNK), :], axis=1, keepdims=True), (CHUNK, BLK)
+        )
 
         def weigh(slot, c2):
-            w = jnp.exp(s_sc[slot, pl.ds(r0, CHUNK), :] - m).astype(jnp.bfloat16)
-            vb = got[slot // LEVEL, slot % LEVEL, 1]
-            num_sc[pl.ds(r0, CHUNK), :] += jnp.dot(w, vb, preferred_element_type=jnp.float32)
-            den_sc[pl.ds(r0, CHUNK), :] += w.astype(jnp.float32)
+            d = LEVEL * (slot // LEVEL) + q - slot % LEVEL
+
+            @pl.when((d >= 0) & (d < WMAX) & (g >= d))
+            def _():
+                w = jnp.exp(s_sc[slot, pl.ds(r0, CHUNK), :] - m_sc[pl.ds(r0, CHUNK), :]).astype(jnp.bfloat16)
+                vb = got[slot // LEVEL, slot % LEVEL, 1]
+                num_sc[pl.ds(r0, CHUNK), :] += jnp.dot(w, vb, preferred_element_type=jnp.float32)
+                den_sc[pl.ds(r0, CHUNK), :] += w.astype(jnp.float32)
+
             return c2
 
         lax.fori_loop(0, DEPTH * LEVEL, weigh, 0)
@@ -199,7 +221,7 @@
     doc_here = block_docs[g]
     doc_there = jnp.take(block_docs, jnp.clip(key_block, 0, block_docs.shape[0] - 1))
     ok = (dist >= 0) & (dist < WMAX) & (key_block >= 0) & (doc_there == doc_here)
-    win_rows = jnp.broadcast_to(jnp.tile(windows, rows_here)[:, None], (rows_here * heads, BLK))
+    win_rows = jnp.broadcast_to(windows[:, None], (heads, BLK))
     out = fused(ok.astype(jnp.int32), kv, queries.reshape(rows_here * heads, hd), win_rows, n_ctx, n_sub)
     return out.reshape(rows_here, heads, hd)
 

time: 101 us -> 104 us (1.030)
  the two profiles are of different devices: /device:TPU:128 before, /device:TPU:47 now
where the time goes in v4:
time: 104 us
  Pallas kernels  97.5 us (94%)
  local copies, waits for them, and re-layouts  4.34 us (4%)
  other arithmetic  1.85 us (2%)
    pallas_call x1, Pallas kernels, fused(): pl.pallas_call(functools.partial(fused_kernel, n_ctx, n_sub), out_shape=j...  97.5 us
    unnamed x9, local copies, waits for them, and re-layouts  2.37 us

profile of v4, /device:TPU:47, one launch (start us, length us, event | category | flops | bytes accessed | tf_op | source)
XLA Modules:
  0.0 103.7 jit_solution(13835927088465150937)
XLA Ops:
  0.0 0.0 copy-start
  0.0 0.7 copy-done
  0.7 0.6 dynamic_slice.3
  1.3 0.0 copy-start.1
  1.3 0.0 copy-start.2
  1.3 0.7 gather_fusion
  2.1 0.0 copy-start.3
  2.1 1.2 %and_convert_fusion.ok_ref = s32[36]{0:T(128)} fusion(s32[36]{0:T(128)S(1)} %gather_fusion, s32[]{:T(128)} %bitcast.1, s32[]{:T(128)S(6)} %add.81, s32[]{:T(128)S(6)} %select_n.63), kind=kLoop, calls=%fused_computation.5 | loop fusion | flops 1152 | bytes 300 | tf_op jit(solution)/shard_map/convert_element_type | solution.py:225
  3.2 0.0 copy-done.3
  3.2 0.7 broadcast_in_dim.13.win_ref
  3.9 0.0 copy-done.1
  3.9 0.0 copy-done.2
  3.9 0.6 pad_maximum_fusion.kv_ref
  4.5 97.5 %shard_map.55 = bf16[1024,128]{1,0:T(8,128)(2,1)} custom-call(s32[36]{0:T(128)} %and_convert_fusion.ok_ref, bf16[2,128,128]{2,1,0:T(8,128)(2,1)} %pad_maximum_fusion.kv_ref, bf16[1024,128]{1,0:T(8,128)(2,1)} %bitcast.8, s32[8,128]{1,0:T(8,128)} %broadcast_in_dim.13.win_ref), custom_call_target="tpu_custom_call" | custom-call | tf_op jit(solution)/shard_map/pallas_call | solution.py:178
  102.0 1.7 %copy.7 = bf16[128,8,128]{2,1,0:T(8,128)(2,1)} copy(bf16[128,8,128]{2,1,0:T(8,128)(2,1)} %bitcast.7) | data formatting | bytes 524288
  (2 shorter events, 0.0 us)
Async XLA Ops:
  0.0 0.7 copy-start
  1.3 2.6 %copy-start.1 = (bf16[128,128]{1,0:T(8,128)(2,1)S(1)}, bf16[128,128]{1,0:T(8,128)(2,1)}, u32[]{:S(2)}) copy-start(bf16[128,128]{1,0:T(8,128)(2,1)} %param.7) | copy-start | bytes 98308
  1.3 2.6 %copy-start.2 = (bf16[128,128]{1,0:T(8,128)(2,1)S(1)}, bf16[128,128]{1,0:T(8,128)(2,1)}, u32[]{:S(2)}) copy-start(bf16[128,128]{1,0:T(8,128)(2,1)} %param.6) | copy-start | bytes 98308
  2.1 1.2 %copy-start.3 = (s32[8]{0:T(128)S(1)}, s32[8]{0:T(128)}, u32[]{:S(2)}) copy-start(s32[8]{0:T(128)} %param.9) | copy-start | bytes 100

commit v5 on v2

--- a/solution.py
+++ b/solution.py
@@ -97,81 +97,52 @@
     )(kv)
 
 
-def attend_kernel(ok_ref, dist_ref, q_ref, got_ref, win_ref, out_ref, s_sc, m_sc, num_sc, den_sc):
+def attend_kernel(q_ref, k_ref, v_ref, bias_ref, own_ref, out_ref, s_sc):
     rows, hd = q_ref.shape
-    chunk = s_sc.shape[1]
-    slots = s_sc.shape[0]
-    heads = rows // BLK
+    chunk, keys = s_sc.shape
+    heads = bias_ref.shape[0]
     scale = hd ** -0.5
+    own = pl.multiple_of(own_ref[0] * BLK, BLK)
+    ones = jnp.ones((keys, BLK), jnp.bfloat16)
 
     def one_chunk(ci, carry):
         r0 = pl.multiple_of(ci * chunk, chunk)
         qc = q_ref[pl.ds(r0, chunk), :]
+        sc = lax.dot_general(qc, k_ref[...], (((1,), (1,)), ((), ())), preferred_element_type=jnp.float32) * scale
+        sc = (sc.reshape(chunk // heads, heads, keys) + bias_ref[...][None]).reshape(chunk, keys)
+        s_sc[...] = sc
         query_i = (lax.broadcasted_iota(jnp.int32, (chunk, BLK), 0) + r0) // heads
         key_j = lax.broadcasted_iota(jnp.int32, (chunk, BLK), 1)
-        causal = key_j <= query_i
-        m_sc[...] = jnp.full(m_sc.shape, -jnp.inf, jnp.float32)
-        num_sc[...] = jnp.zeros(num_sc.shape, jnp.float32)
-        den_sc[...] = jnp.zeros(den_sc.shape, jnp.float32)
-
-        def first(slot, c2):
-            d = dist_ref[slot]
-
-            @pl.when(ok_ref[slot] != 0)
-            def _():
-                kb = got_ref[slot // LEVEL, slot % LEVEL, 0]
-                sc = lax.dot_general(qc, kb, (((1,), (1,)), ((), ())), preferred_element_type=jnp.float32) * scale
-                allowed = (win_ref[pl.ds(r0, chunk), :] > d) & (causal | (d > 0))
-                sc = jnp.where(allowed, sc, -jnp.inf)
-                s_sc[slot] = sc
-                m_sc[...] = jnp.maximum(m_sc[...], sc)
-
-            return c2
-
-        lax.fori_loop(0, slots, first, 0)
-        m = jnp.max(m_sc[...], axis=1, keepdims=True)
-
-        def second(slot, c2):
-            @pl.when(ok_ref[slot] != 0)
-            def _():
-                w = jnp.exp(s_sc[slot] - m).astype(jnp.bfloat16)
-                vb = got_ref[slot // LEVEL, slot % LEVEL, 1]
-                num_sc[...] += jnp.dot(w, vb, preferred_element_type=jnp.float32)
-                den_sc[...] += w.astype(jnp.float32)
-
-            return c2
-
-        lax.fori_loop(0, slots, second, 0)
-        den = jnp.sum(den_sc[...], axis=1, keepdims=True)
-        out_ref[pl.ds(r0, chunk), :] = (num_sc[...] / den).astype(out_ref.dtype)
+        s_sc[:, pl.ds(own, BLK)] = jnp.where(key_j <= query_i, s_sc[:, pl.ds(own, BLK)], -jnp.inf)
+        sc = s_sc[...]
+        m = jnp.max(sc, axis=1, keepdims=True)
+        w = jnp.exp(sc - m).astype(jnp.bfloat16)
+        num = jnp.dot(w, v_ref[...], preferred_element_type=jnp.float32)
+        den = jnp.dot(w, ones, preferred_element_type=jnp.float32)
+        out_ref[pl.ds(r0, chunk), :] = (num / den[:, :1]).astype(out_ref.dtype)
         return carry
 
     lax.fori_loop(0, rows // chunk, one_chunk, 0)
 
 
-def attend(ok, dist, q2, got, win_rows):
+def attend(q2, k_all, v_all, bias, own):
     rows, hd = q2.shape
-    chunk = 512
-    slots = DEPTH * LEVEL
+    keys = k_all.shape[0]
+    chunk = 256
     return pl.pallas_call(
         attend_kernel,
         out_shape=jax.ShapeDtypeStruct((rows, hd), q2.dtype),
         in_specs=[
-            pl.BlockSpec(memory_space=pltpu.SMEM),
-            pl.BlockSpec(memory_space=pltpu.SMEM),
             pl.BlockSpec(memory_space=pltpu.VMEM),
             pl.BlockSpec(memory_space=pltpu.VMEM),
             pl.BlockSpec(memory_space=pltpu.VMEM),
+            pl.BlockSpec(memory_space=pltpu.VMEM),
+            pl.BlockSpec(memory_space=pltpu.SMEM),
         ],
         out_specs=pl.BlockSpec(memory_space=pltpu.VMEM),
-        scratch_shapes=[
-            pltpu.VMEM((slots, chunk, BLK), jnp.float32),
-            pltpu.VMEM((chunk, BLK), jnp.float32),
-            pltpu.VMEM((chunk, hd), jnp.float32),
-            pltpu.VMEM((chunk, BLK), jnp.float32),
-        ],
+        scratch_shapes=[pltpu.VMEM((chunk, keys), jnp.float32)],
         compiler_params=pltpu.CompilerParams(vmem_limit_bytes=48 * 1024 * 1024),
-    )(ok, dist, q2, got, win_rows)
+    )(q2, k_all, v_all, bias, own)
 
 
 def local(queries, key_rows, value_rows, block_docs, windows):
@@ -184,16 +155,21 @@
     rows_here, heads, hd = queries.shape
     kv = jnp.stack([key_rows, value_rows])
     got = relay(kv, n_ctx, n_sub)
+    slots = DEPTH * LEVEL
+    k_all = got[:, :, 0].reshape(slots * BLK, hd)
+    v_all = got[:, :, 1].reshape(slots * BLK, hd)
 
-    k_of = jnp.arange(DEPTH * LEVEL, dtype=jnp.int32) // LEVEL
-    col_of = jnp.arange(DEPTH * LEVEL, dtype=jnp.int32) % LEVEL
+    k_of = jnp.arange(slots, dtype=jnp.int32) // LEVEL
+    col_of = jnp.arange(slots, dtype=jnp.int32) % LEVEL
     dist = LEVEL * k_of + q - col_of
     key_block = g - dist
     doc_here = block_docs[g]
     doc_there = jnp.take(block_docs, jnp.clip(key_block, 0, block_docs.shape[0] - 1))
     ok = (dist >= 0) & (dist < WMAX) & (key_block >= 0) & (doc_there == doc_here)
-    win_rows = jnp.broadcast_to(jnp.tile(windows, rows_here)[:, None], (rows_here * heads, BLK))
-    out = attend(ok.astype(jnp.int32), dist, queries.reshape(rows_here * heads, hd), got, win_rows)
+    allowed = ok[None, :] & (windows[:, None] > dist[None, :])
+    bias = jnp.repeat(jnp.where(allowed, 0.0, -jnp.inf).astype(jnp.float32), BLK, axis=1)
+    own = jnp.reshape(q, (1,)).astype(jnp.int32)
+    out = attend(queries.reshape(rows_here * heads, hd), k_all, v_all, bias, own)
     return out.reshape(rows_here, heads, hd)
 
 

time: 91 us -> 71.2 us (0.78)
  Pallas kernels: 83.1 us -> 65.3 us
  local copies, waits for them, and re-layouts: 5.38 us -> 3.38 us
    pallas_call x1, Pallas kernels: 29.2 us -> 11.4 us  [attend(): pl.pallas_call(attend_kernel, out_shape=jax.ShapeDtypeStruct((rows, hd),...]
    slice x0 -> x1, local copies, waits for them, and re-layouts: none -> 1.94 us  [local(): v_all = got[:, :, 1].reshape(slots * BLK, hd)]
    unnamed x4 -> x6, local copies, waits for them, and re-layouts: 1.66 us -> 0.02 us
where the time goes in v5:
time: 71.2 us; the launch traced here: 71 us
  Pallas kernels  65.3 us (92%)
  local copies, waits for them, and re-layouts  3.38 us (5%)
  other arithmetic  2.17 us (3%)
    pallas_call x1, Pallas kernels, relay(): pl.pallas_call(functools.partial(relay_kernel, n_ctx, n_sub), out_shape=j...  53.9 us
    pallas_call x1, Pallas kernels, attend(): pl.pallas_call(attend_kernel, out_shape=jax.ShapeDtypeStruct((rows, hd),...  11.4 us
    slice x1, local copies, waits for them, and re-layouts, local(): v_all = got[:, :, 1].reshape(slots * BLK, hd)  1.94 us

profile of v5, /device:TPU:63, one launch (start us, length us, event | category | flops | bytes accessed | tf_op | source)
XLA Modules:
  0.0 71.0 jit_solution(1301864869732428334)
XLA Ops:
  0.0 1.4 %pad_maximum_fusion.kv_ref = bf16[2,128,128]{2,1,0:T(8,128)(2,1)} fusion(bf16[1,128,128]{2,1,0:T(8,128)(2,1)} %bitcast.15, bf16[1,128,128]{2,1,0:T(8,128)(2,1)} %bitcast.16), kind=kLoop, calls=%fused_computation.2 | loop fusion | flops 32768 | bytes 131072 | tf_op jit(solution)/shard_map/stack | solution.py:156
  1.4 53.9 %shard_map.55 = bf16[9,4,2,128,128]{4,3,2,1,0:T(8,128)(2,1)} custom-call(bf16[2,128,128]{2,1,0:T(8,128)(2,1)} %pad_maximum_fusion.kv_ref), custom_call_target="tpu_custom_call" | custom-call | tf_op jit(solution)/shard_map/pallas_call | solution.py:83
  55.3 0.0 copy-start.1
  55.4 0.0 copy-start.2
  55.4 0.0 copy-start
  55.4 1.9 %fusion.9 = (bf16[9,4,1,128,128]{4,3,2,1,0:T(8,128)(2,1)S(1)}, bf16[9,4,1,128,128]{4,3,2,1,0:T(8,128)(2,1)S(1)}) fusion(bf16[9,4,2,128,128]{4,3,2,1,0:T(8,128)(2,1)} %shard_map.55), kind=kLoop, calls=%fused_computation.28 | loop fusion | bytes 4718592 | tf_op jit(solution)/shard_map/slice | solution.py:160
  57.4 0.0 copy-done.1
  57.4 0.7 %gather_fusion = s32[36]{0:T(128)S(1)} fusion(s32[768]{0:T(1024)S(1)} %copy-done.1, s32[1024]{0:T(1024)S(1)} %pad_clamp_fusion), kind=kCustom, calls=%fused_computation | custom fusion | bytes 432 | tf_op jit(solution)/shard_map/jit(_take)/gather | solution.py:167
  58.2 0.6 dynamic_slice.3
  58.7 0.7 compare_and_fusion
  59.4 0.0 copy-done.2
  59.4 0.1 and_select_fusion
  59.5 0.1 broadcast_bitcast_fusion.bias_ref
  59.6 0.0 copy-done
  59.6 11.4 %shard_map.56 = bf16[1024,128]{1,0:T(8,128)(2,1)} custom-call(bf16[1024,128]{1,0:T(8,128)(2,1)S(1)} %bitcast.14, bf16[4608,128]{1,0:T(8,128)(2,1)S(1)} %bitcast.13, bf16[4608,128]{1,0:T(8,128)(2,1)S(1)} %bitcast.12, f32[8,4608]{1,0:T(8,128)S(1)} %broadcast_bitcast_fusion.bias_ref, s32[1]{0:T(128)} %bitcast.8.own_ref), custom_call_target="tpu_custom_call" | custom-call | tf_op jit(solution)/shard_map/pallas_call | solution.py:132
  (3 shorter events, 0.0 us)
Async XLA Ops:
  55.3 2.1 %copy-start.1 = (s32[768]{0:T(1024)S(1)}, s32[768]{0:T(1024)}, u32[]{:S(2)}) copy-start(s32[768]{0:T(1024)} %param.8) | copy-start | bytes 9220
  55.4 4.1 %copy-start.2 = (s32[8]{0:T(128)S(1)}, s32[8]{0:T(128)}, u32[]{:S(2)}) copy-start(s32[8]{0:T(128)} %param.9) | copy-start | bytes 100
  55.4 4.2 %copy-start = (bf16[128,8,128]{2,1,0:T(8,128)(2,1)S(1)}, bf16[128,8,128]{2,1,0:T(8,128)(2,1)}, u32[]{:S(2)}) copy-start(bf16[128,8,128]{2,1,0:T(8,128)(2,1)} %param.5) | copy-start | bytes 786436

commit v6 on v5

--- a/solution.py
+++ b/solution.py
@@ -14,7 +14,7 @@
 MESH = pl.DeviceIdType.MESH
 
 
-def relay_kernel(n_ctx, n_sub, kv_ref, got_ref, recv_sem, relay_sem, sib_sem, cross_sem, fwd_sem, own_sem):
+def relay_kernel(n_ctx, n_sub, k_ref, v_ref, got_k, got_v, recv_sem, relay_sem, sib_sem, cross_sem, fwd_sem, own_sem):
     c = lax.axis_index("ctx")
     s = lax.axis_index("sub")
     total = n_ctx * n_sub
@@ -26,75 +26,89 @@
     pred = (pred_g // n_sub, pred_g % n_sub)
     sib_q = q + 1 - 2 * (q % 2)
     cross_q = q + 2 - 4 * ((q // 2) % 2)
+    far_q = 3 - q
     sib = (c, s - q + sib_q)
     cross = (c, s - q + cross_q)
+    planes = (got_k, got_v)
+    inputs = (k_ref, v_ref)
 
     barrier = pltpu.get_barrier_semaphore()
     for peer in (succ, pred, sib, cross):
         pl.semaphore_signal(barrier, inc=1, device_id=peer, device_id_type=MESH)
     pl.semaphore_wait(barrier, 4)
 
-    own = pltpu.make_async_copy(kv_ref, got_ref.at[0, q], own_sem.at[0])
-    own.start()
+    owns = [pltpu.make_async_copy(inputs[p], planes[p].at[0, q], own_sem.at[p]) for p in range(2)]
+    for cp in owns:
+        cp.start()
 
-    def remote(src, k, col, peer, sem):
+    def remote(p, src, k, col, peer, sem):
         return pltpu.make_async_remote_copy(
             src_ref=src,
-            dst_ref=got_ref.at[k, col],
-            send_sem=sem,
-            recv_sem=recv_sem.at[k, col],
+            dst_ref=planes[p].at[k, col],
+            send_sem=sem.at[p],
+            recv_sem=recv_sem.at[p, k, col],
             device_id=peer,
             device_id_type=MESH,
         )
 
+    def source(p, k, col):
+        return inputs[p] if k == 0 else planes[p].at[k, col]
+
     sends = []
     for k in range(DEPTH):
-        src = kv_ref if k == 0 else got_ref.at[k, q]
         if k > 0:
-            remote(src, k, q, pred, relay_sem.at[k - 1]).wait_recv()
+            for p in range(2):
+                remote(p, source(p, k, q), k, q, pred, relay_sem.at[k - 1]).wait_recv()
         if k + 1 < DEPTH:
-            cp = remote(src, k + 1, q, succ, relay_sem.at[k])
+            for p in range(2):
+                cp = remote(p, source(p, k, q), k + 1, q, succ, relay_sem.at[k])
+                cp.start()
+                sends.append(cp)
+        for p in range(2):
+            cp = remote(p, source(p, k, q), k, q, cross, cross_sem.at[k])
             cp.start()
             sends.append(cp)
-        cp = remote(src, k, q, cross, cross_sem.at[k])
-        cp.start()
-        sends.append(cp)
-        cp = remote(src, k, q, sib, sib_sem.at[k])
-        cp.start()
-        sends.append(cp)
+        for p in range(2):
+            cp = remote(p, source(p, k, q), k, q, sib, sib_sem.at[k])
+            cp.start()
+            sends.append(cp)
 
     for k in range(DEPTH):
-        got_cross = got_ref.at[k, cross_q]
-        remote(got_cross, k, cross_q, cross, cross_sem.at[k]).wait_recv()
-        cp = remote(got_cross, k, cross_q, sib, fwd_sem.at[k])
-        cp.start()
-        sends.append(cp)
+        for p in range(2):
+            got_cross = planes[p].at[k, cross_q]
+            remote(p, got_cross, k, cross_q, cross, cross_sem.at[k]).wait_recv()
+            cp = remote(p, got_cross, k, cross_q, sib, fwd_sem.at[k])
+            cp.start()
+            sends.append(cp)
 
-    far_q = 3 - q
     for k in range(DEPTH):
-        remote(got_ref.at[k, sib_q], k, sib_q, sib, sib_sem.at[k]).wait_recv()
-        remote(got_ref.at[k, far_q], k, far_q, sib, fwd_sem.at[k]).wait_recv()
+        for p in range(2):
+            remote(p, planes[p].at[k, sib_q], k, sib_q, sib, sib_sem.at[k]).wait_recv()
+        for p in range(2):
+            remote(p, planes[p].at[k, far_q], k, far_q, sib, fwd_sem.at[k]).wait_recv()
     for cp in sends:
         cp.wait_send()
-    own.wait()
+    for cp in owns:
+        cp.wait()
 
 
-def relay(kv, n_ctx, n_sub):
+def relay(key_rows, value_rows, n_ctx, n_sub):
+    plane = jax.ShapeDtypeStruct((DEPTH, LEVEL) + key_rows.shape, key_rows.dtype)
     return pl.pallas_call(
         functools.partial(relay_kernel, n_ctx, n_sub),
-        out_shape=jax.ShapeDtypeStruct((DEPTH, LEVEL) + kv.shape, kv.dtype),
-        in_specs=[pl.BlockSpec(memory_space=pltpu.VMEM)],
-        out_specs=pl.BlockSpec(memory_space=pl.ANY),
+        out_shape=(plane, plane),
+        in_specs=[pl.BlockSpec(memory_space=pltpu.VMEM)] * 2,
+        out_specs=(pl.BlockSpec(memory_space=pl.ANY), pl.BlockSpec(memory_space=pl.ANY)),
         scratch_shapes=[
-            pltpu.SemaphoreType.DMA((DEPTH, LEVEL)),
-            pltpu.SemaphoreType.DMA((DEPTH,)),
-            pltpu.SemaphoreType.DMA((DEPTH,)),
-            pltpu.SemaphoreType.DMA((DEPTH,)),
-            pltpu.SemaphoreType.DMA((DEPTH,)),
-            pltpu.SemaphoreType.DMA((1,)),
+            pltpu.SemaphoreType.DMA((2, DEPTH, LEVEL)),
+            pltpu.SemaphoreType.DMA((DEPTH, 2)),
+            pltpu.SemaphoreType.DMA((DEPTH, 2)),
+            pltpu.SemaphoreType.DMA((DEPTH, 2)),
+            pltpu.SemaphoreType.DMA((DEPTH, 2)),
+            pltpu.SemaphoreType.DMA((2,)),
         ],
         compiler_params=pltpu.CompilerParams(collective_id=0, has_side_effects=True),
-    )(kv)
+    )(key_rows, value_rows)
 
 
 def attend_kernel(q_ref, k_ref, v_ref, bias_ref, own_ref, out_ref, s_sc):
@@ -153,11 +167,10 @@
     g = c * n_sub + s
     q = s % LEVEL
     rows_here, heads, hd = queries.shape
-    kv = jnp.stack([key_rows, value_rows])
-    got = relay(kv, n_ctx, n_sub)
+    got_k, got_v = relay(key_rows, value_rows, n_ctx, n_sub)
     slots = DEPTH * LEVEL
-    k_all = got[:, :, 0].reshape(slots * BLK, hd)
-    v_all = got[:, :, 1].reshape(slots * BLK, hd)
+    k_all = got_k.reshape(slots * BLK, hd)
+    v_all = got_v.reshape(slots * BLK, hd)
 
     k_of = jnp.arange(slots, dtype=jnp.int32) // LEVEL
     col_of = jnp.arange(slots, dtype=jnp.int32) % LEVEL

time: 71.2 us -> 74.1 us (1.041)
  local copies, waits for them, and re-layouts: 3.38 us -> 6.31 us
  other arithmetic: 2.17 us -> 1.42 us
    unnamed x6, local copies, waits for them, and re-layouts: 0.02 us -> 3.48 us
    slice x1 -> x0, local copies, waits for them, and re-layouts: 1.94 us -> none  [local(): v_all = got[:, :, 1].reshape(slots * BLK, hd)]
    another operation x1 -> x0, other arithmetic: 1.41 us -> none  [local(): kv = jnp.stack([key_rows, value_rows])]
where the time goes in v6:
time: 74.1 us; the launch traced here: 73.7 us
  Pallas kernels  65.9 us (89%)
  local copies, waits for them, and re-layouts  6.31 us (9%)
  other arithmetic  1.42 us (2%)
    pallas_call x1, Pallas kernels, relay(): pl.pallas_call(functools.partial(relay_kernel, n_ctx, n_sub), out_shape=(...  54.5 us
    pallas_call x1, Pallas kernels, attend(): pl.pallas_call(attend_kernel, out_shape=jax.ShapeDtypeStruct((rows, hd),...  11.4 us
    unnamed x6, local copies, waits for them, and re-layouts  3.48 us

profile of v6, /device:TPU:63, one launch (start us, length us, event | category | flops | bytes accessed | tf_op | source)
XLA Modules:
  0.0 73.7 jit_solution(8597743912726773218)
XLA Ops:
  0.0 1.3 %dynamic_slice.3 = s32[1]{0:T(128)} dynamic-slice(s32[768]{0:T(1024)} %param.8, s32[]{:T(128)S(6)} %select_n.98), dynamic_slice_sizes={1} | dynamic-slice | bytes 12 | tf_op jit(solution)/shard_map/dynamic_slice | solution.py:179
  1.3 1.5 %gather_fusion = s32[36]{0:T(128)S(1)} fusion(s32[768]{0:T(1024)} %param.8, s32[1024]{0:T(1024)S(1)} %pad_clamp_fusion), kind=kCustom, calls=%fused_computation | custom fusion | bytes 432 | tf_op jit(solution)/shard_map/jit(_take)/gather | solution.py:180
  2.8 0.7 compare_and_fusion
  3.4 0.7 and_select_fusion
  4.2 0.1 broadcast_bitcast_fusion.bias_ref
  4.3 54.5 %shard_map.55 = (bf16[9,4,128,128]{3,2,1,0:T(8,128)(2,1)}, bf16[9,4,128,128]{3,2,1,0:T(8,128)(2,1)}) custom-call(bf16[128,128]{1,0:T(8,128)(2,1)} %k_ref.1, bf16[128,128]{1,0:T(8,128)(2,1)} %v_ref.1), custom_call_target="tpu_custom_call" | custom-call | tf_op jit(solution)/shard_map/pallas_call | solution.py:97
  58.8 0.0 copy-start
  58.8 1.3 %copy-done = bf16[9,4,128,128]{3,2,1,0:T(8,128)(2,1)S(1)} copy-done((bf16[9,4,128,128]{3,2,1,0:T(8,128)(2,1)S(1)}, bf16[9,4,128,128]{3,2,1,0:T(8,128)(2,1)}, u32[]{:S(2)}) %copy-start) | copy-done | bytes 1179672
  60.1 0.0 copy-start.1
  60.1 1.3 %copy-done.1 = bf16[9,4,128,128]{3,2,1,0:T(8,128)(2,1)S(1)} copy-done((bf16[9,4,128,128]{3,2,1,0:T(8,128)(2,1)S(1)}, bf16[9,4,128,128]{3,2,1,0:T(8,128)(2,1)}, u32[]{:S(2)}) %copy-start.1) | copy-done | bytes 1179672
  61.4 0.0 copy-start.2
  61.4 0.9 %copy-done.2 = bf16[128,8,128]{2,1,0:T(8,128)(2,1)S(1)} copy-done((bf16[128,8,128]{2,1,0:T(8,128)(2,1)S(1)}, bf16[128,8,128]{2,1,0:T(8,128)(2,1)}, u32[]{:S(2)}) %copy-start.2) | copy-done | bytes 262168
  62.3 11.4 %shard_map.56 = bf16[1024,128]{1,0:T(8,128)(2,1)} custom-call(bf16[1024,128]{1,0:T(8,128)(2,1)S(1)} %bitcast.12, bf16[4608,128]{1,0:T(8,128)(2,1)S(1)} %bitcast.10, bf16[4608,128]{1,0:T(8,128)(2,1)S(1)} %bitcast.11, f32[8,4608]{1,0:T(8,128)S(1)} %broadcast_bitcast_fusion.bias_ref, s32[1]{0:T(128)} %bitcast.6.own_ref), custom_call_target="tpu_custom_call" | custom-call | tf_op jit(solution)/shard_map/pallas_call | solution.py:146
  (3 shorter events, 0.0 us)
Async XLA Ops:
  58.8 1.3 %copy-start = (bf16[9,4,128,128]{3,2,1,0:T(8,128)(2,1)S(1)}, bf16[9,4,128,128]{3,2,1,0:T(8,128)(2,1)}, u32[]{:S(2)}) copy-start(bf16[9,4,128,128]{3,2,1,0:T(8,128)(2,1)} %get-tuple-element.7) | copy-start | bytes 3538948
  60.1 1.3 %copy-start.1 = (bf16[9,4,128,128]{3,2,1,0:T(8,128)(2,1)S(1)}, bf16[9,4,128,128]{3,2,1,0:T(8,128)(2,1)}, u32[]{:S(2)}) copy-start(bf16[9,4,128,128]{3,2,1,0:T(8,128)(2,1)} %get-tuple-element.8) | copy-start | bytes 3538948
  61.4 0.9 %copy-start.2 = (bf16[128,8,128]{2,1,0:T(8,128)(2,1)S(1)}, bf16[128,8,128]{2,1,0:T(8,128)(2,1)}, u32[]{:S(2)}) copy-start(bf16[128,8,128]{2,1,0:T(8,128)(2,1)} %param.5) | copy-start | bytes 786436

commit v7 on v6

v7 whole, which is shorter than its diff:
```python
import functools

import jax
import jax.numpy as jnp
from jax import lax
from jax.experimental import pallas as pl
from jax.experimental.pallas import tpu as pltpu
from jax.sharding import PartitionSpec as P

BLK = 128
WMAX = 32
LEVEL = 4
DEPTH = (WMAX - 1 + LEVEL - 1) // LEVEL + 1
MESH = pl.DeviceIdType.MESH


def fused_kernel(n_ctx, n_sub, docs_ref, win_ref, k_ref, v_ref, q_ref, out_ref,
                 got_k, got_v, bias_sc, s_sc, recv_sem, relay_sem, sib_sem, cross_sem, fwd_sem, own_sem):
    c = lax.axis_index("ctx")
    s = lax.axis_index("sub")
    total = n_ctx * n_sub
    g = c * n_sub + s
    q = s % LEVEL
    succ_g = (g + LEVEL) % total
    pred_g = (g + total - LEVEL) % total
    succ = (succ_g // n_sub, succ_g % n_sub)
    pred = (pred_g // n_sub, pred_g % n_sub)
    sib_q = q + 1 - 2 * (q % 2)
    cross_q = q + 2 - 4 * ((q // 2) % 2)
    far_q = 3 - q
    sib = (c, s - q + sib_q)
    cross = (c, s - q + cross_q)
    planes = (got_k, got_v)
    inputs = (k_ref, v_ref)
    rows, hd = q_ref.shape
    chunk, keys = s_sc.shape
    heads = bias_sc.shape[0]
    n_blocks = docs_ref.shape[0]

    def at(p, k, col):
        return planes[p].at[pl.ds(pl.multiple_of((k * LEVEL + col) * BLK, BLK), BLK)]

    barrier = pltpu.get_barrier_semaphore()
    for peer in (succ, pred, sib, cross):
        pl.semaphore_signal(barrier, inc=1, device_id=peer, device_id_type=MESH)
    pl.semaphore_wait(barrier, 4)

    owns = [pltpu.make_async_copy(inputs[p], at(p, 0, q), own_sem.at[p]) for p in range(2)]
    for cp in owns:
        cp.start()

    def remote(p, src, k, col, peer, sem):
        return pltpu.make_async_remote_copy(
            src_ref=src,
            dst_ref=at(p, k, col),
            send_sem=sem.at[p],
            recv_sem=recv_sem.at[p, k, col],
            device_id=peer,
            device_id_type=MESH,
        )

    def source(p, k, col):
        return inputs[p] if k == 0 else at(p, k, col)

    sends = []
    for k in range(DEPTH):
        if k > 0:
            for p in range(2):
                remote(p, source(p, k, q), k, q, pred, relay_sem.at[k - 1]).wait_recv()
        if k + 1 < DEPTH:
            for p in range(2):
                cp = remote(p, source(p, k, q), k + 1, q, succ, relay_sem.at[k])
                cp.start()
                sends.append(cp)
        for p in range(2):
            cp = remote(p, source(p, k, q), k, q, cross, cross_sem.at[k])
            cp.start()
            sends.append(cp)
        for p in range(2):
            cp = remote(p, source(p, k, q), k, q, sib, sib_sem.at[k])
            cp.start()
            sends.append(cp)
        if k == 0:
            head = lax.broadcasted_iota(jnp.int32, (heads, BLK), 0)
            win8 = jnp.zeros((heads, BLK), jnp.int32)
            for h in range(heads):
                win8 = jnp.where(head == h, win_ref[h], win8)
            doc_here = docs_ref[g]
            for slot in range(DEPTH * LEVEL):
                d = LEVEL * (slot // LEVEL) + q - slot % LEVEL
                kb = g - d
                doc_there = docs_ref[(kb + n_blocks) % n_blocks]
                live = (d >= 0) & (d < WMAX) & (kb >= 0) & (doc_there == doc_here)
                keep = (win8 > d) & (jnp.full((heads, BLK), live.astype(jnp.int32)) > 0)
                bias_sc[:, pl.ds(slot * BLK, BLK)] = jnp.where(keep, 0.0, -jnp.inf).astype(jnp.float32)

    for k in range(DEPTH):
        for p in range(2):
            got_cross = at(p, k, cross_q)
            remote(p, got_cross, k, cross_q, cross, cross_sem.at[k]).wait_recv()
            cp = remote(p, got_cross, k, cross_q, sib, fwd_sem.at[k])
            cp.start()
            sends.append(cp)

    for k in range(DEPTH):
        for p in range(2):
            remote(p, at(p, k, sib_q), k, sib_q, sib, sib_sem.at[k]).wait_recv()
        for p in range(2):
            remote(p, at(p, k, far_q), k, far_q, sib, fwd_sem.at[k]).wait_recv()
    for cp in owns:
        cp.wait()

    scale = hd ** -0.5
    own = pl.multiple_of(q * BLK, BLK)
    ones = jnp.ones((keys, BLK), jnp.bfloat16)

    def one_chunk(ci, carry):
        r0 = pl.multiple_of(ci * chunk, chunk)
        qc = q_ref[pl.ds(r0, chunk), :]
        sc = lax.dot_general(qc, got_k[...], (((1,), (1,)), ((), ())), preferred_element_type=jnp.float32) * scale
        sc = (sc.reshape(chunk // heads, heads, keys) + bias_sc[...][None]).reshape(chunk, keys)
        s_sc[...] = sc
        query_i = (lax.broadcasted_iota(jnp.int32, (chunk, BLK), 0) + r0) // heads
        key_j = lax.broadcasted_iota(jnp.int32, (chunk, BLK), 1)
        s_sc[:, pl.ds(own, BLK)] = jnp.where(key_j <= query_i, s_sc[:, pl.ds(own, BLK)], -jnp.inf)
        sc = s_sc[...]
        m = jnp.max(sc, axis=1, keepdims=True)
        w = jnp.exp(sc - m).astype(jnp.bfloat16)
        num = jnp.dot(w, got_v[...], preferred_element_type=jnp.float32)
        den = jnp.dot(w, ones, preferred_element_type=jnp.float32)
        out_ref[pl.ds(r0, chunk), :] = (num / den[:, :1]).astype(out_ref.dtype)
        return carry

    lax.fori_loop(0, rows // chunk, one_chunk, 0)

    for cp in sends:
        cp.wait_send()


def fused(block_docs, windows, key_rows, value_rows, q2, n_ctx, n_sub):
    rows, hd = q2.shape
    keys = DEPTH * LEVEL * BLK
    chunk = 256
    heads = windows.shape[0]
    return pl.pallas_call(
        functools.partial(fused_kernel, n_ctx, n_sub),
        out_shape=jax.ShapeDtypeStruct((rows, hd), q2.dtype),
        in_specs=[
            pl.BlockSpec(memory_space=pltpu.SMEM),
            pl.BlockSpec(memory_space=pltpu.SMEM),
            pl.BlockSpec(memory_space=pltpu.VMEM),
            pl.BlockSpec(memory_space=pltpu.VMEM),
            pl.BlockSpec(memory_space=pltpu.VMEM),
        ],
        out_specs=pl.BlockSpec(memory_space=pltpu.VMEM),
        scratch_shapes=[
            pltpu.VMEM((keys, hd), key_rows.dtype),
            pltpu.VMEM((keys, hd), value_rows.dtype),
            pltpu.VMEM((heads, keys), jnp.float32),
            pltpu.VMEM((chunk, keys), jnp.float32),
            pltpu.SemaphoreType.DMA((2, DEPTH, LEVEL)),
            pltpu.SemaphoreType.DMA((DEPTH, 2)),
            pltpu.SemaphoreType.DMA((DEPTH, 2)),
            pltpu.SemaphoreType.DMA((DEPTH, 2)),
            pltpu.SemaphoreType.DMA((DEPTH, 2)),
            pltpu.SemaphoreType.DMA((2,)),
        ],
        compiler_params=pltpu.CompilerParams(
            collective_id=0, has_side_effects=True, vmem_limit_bytes=48 * 1024 * 1024
        ),
    )(block_docs, windows, key_rows, value_rows, q2)


def local(queries, key_rows, value_rows, block_docs, windows):
    n_ctx = lax.axis_size("ctx")
    n_sub = lax.axis_size("sub")
    rows_here, heads, hd = queries.shape
    out = fused(block_docs, windows, key_rows, value_rows, queries.reshape(rows_here * heads, hd), n_ctx, n_sub)
    return out.reshape(rows_here, heads, hd)


def solution(mesh):
    in_specs = (
        P(("ctx", "sub"), None, None),
        P(("ctx", "sub"), None),
        P(("ctx", "sub"), None),
        P(),
        P(),
    )
    out_specs = P(("ctx", "sub"), None, None)
    return jax.shard_map(local, mesh=mesh, in_specs=in_specs, out_specs=out_specs, check_vma=False)
```

time: 74.1 us -> 69.5 us (0.938)
  the two profiles are of different devices: /device:TPU:63 before, /device:TPU:47 now
where the time goes in v7:
time: 69.5 us; the launch traced here: 69.1 us
  Pallas kernels  64.6 us (93%)
  local copies, waits for them, and re-layouts  4.51 us (6%)
    pallas_call x1, Pallas kernels, fused(): pl.pallas_call(functools.partial(fused_kernel, n_ctx, n_sub), out_shape=j...  64.6 us
    unnamed x11, local copies, waits for them, and re-layouts  4.51 us

profile of v7, /device:TPU:47, one launch (start us, length us, event | category | flops | bytes accessed | tf_op | source)
XLA Modules:
  0.0 69.1 jit_solution(9134689901067881493)
XLA Ops:
  0.0 0.0 copy-start.4
  0.0 0.7 copy-done.4
  0.7 0.0 copy-start
  0.7 0.9 %copy-done = bf16[128,8,128]{2,1,0:T(8,128)(2,1)S(1)} copy-done((bf16[128,8,128]{2,1,0:T(8,128)(2,1)S(1)}, bf16[128,8,128]{2,1,0:T(8,128)(2,1)}, u32[]{:S(2)}) %copy-start) | copy-done | bytes 262168
  1.6 0.0 copy-start.1
  1.6 0.8 %copy-done.1 = bf16[128,128]{1,0:T(8,128)(2,1)S(1)} copy-done((bf16[128,128]{1,0:T(8,128)(2,1)S(1)}, bf16[128,128]{1,0:T(8,128)(2,1)}, u32[]{:S(2)}) %copy-start.1) | copy-done | bytes 32792
  2.4 0.0 copy-start.2
  2.4 0.8 %copy-done.2 = bf16[128,128]{1,0:T(8,128)(2,1)S(1)} copy-done((bf16[128,128]{1,0:T(8,128)(2,1)S(1)}, bf16[128,128]{1,0:T(8,128)(2,1)}, u32[]{:S(2)}) %copy-start.2) | copy-done | bytes 32792
  3.1 0.0 copy-start.3
  3.1 0.7 copy-done.3
  3.8 64.6 %shard_map.55 = bf16[1024,128]{1,0:T(8,128)(2,1)S(1)} custom-call(s32[768]{0:T(1024)S(1)} %copy-done.3, s32[8]{0:T(128)S(1)} %copy-done.4, bf16[128,128]{1,0:T(8,128)(2,1)S(1)} %copy-done.1, bf16[128,128]{1,0:T(8,128)(2,1)S(1)} %copy-done.2, bf16[1024,128]{1,0:T(8,128)(2,1)S(1)} %bitcast.3), custom_call_target="tpu_custom_call" | custom-call | tf_op jit(solution)/shard_map/pallas_call | solution.py:145
  68.4 0.7 %copy.7 = bf16[128,8,128]{2,1,0:T(8,128)(2,1)} copy(bf16[128,8,128]{2,1,0:T(8,128)(2,1)S(1)} %bitcast.2) | data formatting | bytes 524288
Async XLA Ops:
  0.0 0.7 copy-start.4
  0.7 0.9 %copy-start = (bf16[128,8,128]{2,1,0:T(8,128)(2,1)S(1)}, bf16[128,8,128]{2,1,0:T(8,128)(2,1)}, u32[]{:S(2)}) copy-start(bf16[128,8,128]{2,1,0:T(8,128)(2,1)} %param.5) | copy-start | bytes 786436
  1.6 0.8 %copy-start.1 = (bf16[128,128]{1,0:T(8,128)(2,1)S(1)}, bf16[128,128]{1,0:T(8,128)(2,1)}, u32[]{:S(2)}) copy-start(bf16[128,128]{1,0:T(8,128)(2,1)} %k_ref.1) | copy-start | bytes 98308
  2.4 0.8 %copy-start.2 = (bf16[128,128]{1,0:T(8,128)(2,1)S(1)}, bf16[128,128]{1,0:T(8,128)(2,1)}, u32[]{:S(2)}) copy-start(bf16[128,128]{1,0:T(8,128)(2,1)} %v_ref.1) | copy-start | bytes 98308
  3.1 0.7 copy-start.3

commit v8 on v7

--- a/solution.py
+++ b/solution.py
@@ -14,8 +14,9 @@
 MESH = pl.DeviceIdType.MESH
 
 
-def fused_kernel(n_ctx, n_sub, docs_ref, win_ref, k_ref, v_ref, q_ref, out_ref,
-                 got_k, got_v, bias_sc, s_sc, recv_sem, relay_sem, sib_sem, cross_sem, fwd_sem, own_sem):
+def fused_kernel(n_ctx, n_sub, docs_hbm, win_hbm, k_ref, v_ref, q_hbm, out_ref,
+                 got_k, got_v, bias_sc, s_sc, q_ref, docs_ref, win_ref, in_sem,
+                 recv_sem, relay_sem, sib_sem, cross_sem, fwd_sem, own_sem):
     c = lax.axis_index("ctx")
     s = lax.axis_index("sub")
     total = n_ctx * n_sub
@@ -40,6 +41,14 @@
     def at(p, k, col):
         return planes[p].at[pl.ds(pl.multiple_of((k * LEVEL + col) * BLK, BLK), BLK)]
 
+    loads = [
+        pltpu.make_async_copy(docs_hbm, docs_ref, in_sem.at[0]),
+        pltpu.make_async_copy(win_hbm, win_ref, in_sem.at[1]),
+        pltpu.make_async_copy(q_hbm, q_ref, in_sem.at[2]),
+    ]
+    for cp in loads:
+        cp.start()
+
     barrier = pltpu.get_barrier_semaphore()
     for peer in (succ, pred, sib, cross):
         pl.semaphore_signal(barrier, inc=1, device_id=peer, device_id_type=MESH)
@@ -81,6 +90,8 @@
             cp.start()
             sends.append(cp)
         if k == 0:
+            loads[0].wait()
+            loads[1].wait()
             head = lax.broadcasted_iota(jnp.int32, (heads, BLK), 0)
             win8 = jnp.zeros((heads, BLK), jnp.int32)
             for h in range(heads):
@@ -109,6 +120,7 @@
             remote(p, at(p, k, far_q), k, far_q, sib, fwd_sem.at[k]).wait_recv()
     for cp in owns:
         cp.wait()
+    loads[2].wait()
 
     scale = hd ** -0.5
     own = pl.multiple_of(q * BLK, BLK)
@@ -145,19 +157,17 @@
     return pl.pallas_call(
         functools.partial(fused_kernel, n_ctx, n_sub),
         out_shape=jax.ShapeDtypeStruct((rows, hd), q2.dtype),
-        in_specs=[
-            pl.BlockSpec(memory_space=pltpu.SMEM),
-            pl.BlockSpec(memory_space=pltpu.SMEM),
-            pl.BlockSpec(memory_space=pltpu.VMEM),
-            pl.BlockSpec(memory_space=pltpu.VMEM),
-            pl.BlockSpec(memory_space=pltpu.VMEM),
-        ],
+        in_specs=[pl.BlockSpec(memory_space=pltpu.HBM)] * 5,
         out_specs=pl.BlockSpec(memory_space=pltpu.VMEM),
         scratch_shapes=[
             pltpu.VMEM((keys, hd), key_rows.dtype),
             pltpu.VMEM((keys, hd), value_rows.dtype),
             pltpu.VMEM((heads, keys), jnp.float32),
             pltpu.VMEM((chunk, keys), jnp.float32),
+            pltpu.VMEM((rows, hd), q2.dtype),
+            pltpu.SMEM(block_docs.shape, jnp.int32),
+            pltpu.SMEM(windows.shape, jnp.int32),
+            pltpu.SemaphoreType.DMA((3,)),
             pltpu.SemaphoreType.DMA((2, DEPTH, LEVEL)),
             pltpu.SemaphoreType.DMA((DEPTH, 2)),
             pltpu.SemaphoreType.DMA((DEPTH, 2)),
@@ -166,7 +176,7 @@
             pltpu.SemaphoreType.DMA((2,)),
         ],
         compiler_params=pltpu.CompilerParams(
-            collective_id=0, has_side_effects=True, vmem_limit_bytes=48 * 1024 * 1024
+            collective_id=0, has_side_effects=True, vmem_limit_bytes=67043328
         ),
     )(block_docs, windows, key_rows, value_rows, q2)
 

time: 69.5 us -> 66.8 us (0.961)
  the two profiles are of different devices: /device:TPU:47 before, /device:TPU:63 now
where the time goes in v8:
time: 66.8 us; the launch traced here: 66.6 us
  Pallas kernels  65 us (97%)
  local copies, waits for them, and re-layouts  1.67 us (2%)
    pallas_call x1, Pallas kernels, fused(): pl.pallas_call(functools.partial(fused_kernel, n_ctx, n_sub), out_shape=j...  65 us
    unnamed x1, local copies, waits for them, and re-layouts  1.67 us

profile of v8, /device:TPU:63, one launch (start us, length us, event | category | flops | bytes accessed | tf_op | source)
XLA Modules:
  0.0 66.6 jit_solution(17500435991834962234)
XLA Ops:
  0.0 65.0 %shard_map.55 = bf16[1024,128]{1,0:T(8,128)(2,1)} custom-call(s32[768]{0:T(1024)} %docs_hbm.1, s32[8]{0:T(128)} %win_hbm.1, bf16[128,128]{1,0:T(8,128)(2,1)} %k_ref.1, bf16[128,128]{1,0:T(8,128)(2,1)} %v_ref.1, bf16[1024,128]{1,0:T(8,128)(2,1)} %bitcast.3), custom_call_target="tpu_custom_call" | custom-call | tf_op jit(solution)/shard_map/pallas_call | solution.py:157
  65.0 1.7 %copy.7 = bf16[128,8,128]{2,1,0:T(8,128)(2,1)} copy(bf16[128,8,128]{2,1,0:T(8,128)(2,1)} %bitcast.2) | data formatting | bytes 524288

commit v9 on v8

--- a/solution.py
+++ b/solution.py
@@ -16,7 +16,8 @@
 
 def fused_kernel(n_ctx, n_sub, docs_hbm, win_hbm, k_ref, v_ref, q_hbm, out_ref,
                  got_k, got_v, bias_sc, s_sc, q_ref, docs_ref, win_ref, in_sem,
-                 recv_sem, relay_sem, sib_sem, cross_sem, fwd_sem, own_sem):
+                 recv_sem, relay_sem, sib_sem, cross_sem, fwd_sem, own_sem,
+                 hop_k, hop_v, hop_sem, onward_sem):
     c = lax.axis_index("ctx")
     s = lax.axis_index("sub")
     total = n_ctx * n_sub
@@ -31,6 +32,19 @@
     far_q = 3 - q
     sib = (c, s - q + sib_q)
     cross = (c, s - q + cross_q)
+    z = s // LEVEL
+    last_z = n_sub // LEVEL - 1
+    first = z == 0
+    last = z == last_z
+    next_c = (c + 1) % n_ctx
+    prev_c = (c + n_ctx - 1) % n_ctx
+    last_here = (c, last_z * LEVEL + q)
+    first_here = (c, q)
+    last_next = (next_c, last_z * LEVEL + q)
+    last_prev = (prev_c, last_z * LEVEL + q)
+    first_next = (next_c, q)
+    first_prev = (prev_c, q)
+    hops = (hop_k, hop_v)
     planes = (got_k, got_v)
     inputs = (k_ref, v_ref)
     rows, hd = q_ref.shape
@@ -50,9 +64,34 @@
         cp.start()
 
     barrier = pltpu.get_barrier_semaphore()
-    for peer in (succ, pred, sib, cross):
+
+    def greet(peer):
         pl.semaphore_signal(barrier, inc=1, device_id=peer, device_id_type=MESH)
-    pl.semaphore_wait(barrier, 4)
+
+    greet(sib)
+    greet(cross)
+
+    @pl.when(jnp.logical_not(last))
+    def _():
+        greet(succ)
+
+    @pl.when(jnp.logical_not(first))
+    def _():
+        greet(pred)
+
+    @pl.when(first)
+    def _():
+        greet(first_next)
+        greet(first_prev)
+        greet(last_here)
+
+    @pl.when(last)
+    def _():
+        greet(last_next)
+        greet(last_prev)
+        greet(first_here)
+
+    pl.semaphore_wait(barrier, 4 + 2 * first.astype(jnp.int32) + 2 * last.astype(jnp.int32))
 
     owns = [pltpu.make_async_copy(inputs[p], at(p, 0, q), own_sem.at[p]) for p in range(2)]
     for cp in owns:
@@ -68,19 +107,60 @@
             device_id_type=MESH,
         )
 
+    def hop_at(p, k):
+        return hops[p].at[pl.ds(k * BLK, BLK)]
+
+    def to_hop(p, src, k, peer):
+        return pltpu.make_async_remote_copy(
+            src_ref=src,
+            dst_ref=hop_at(p, k),
+            send_sem=relay_sem.at[k, p],
+            recv_sem=hop_sem.at[p, k],
+            device_id=peer,
+            device_id_type=MESH,
+        )
+
+    def onward(p, k, peer):
+        return pltpu.make_async_remote_copy(
+            src_ref=hop_at(p, k),
+            dst_ref=at(p, k + 1, q),
+            send_sem=onward_sem.at[k, p],
+            recv_sem=recv_sem.at[p, k + 1, q],
+            device_id=peer,
+            device_id_type=MESH,
+        )
+
+    def pass_on(k, peer):
+        for p in range(2):
+            to_hop(p, hop_at(p, k), k, peer).wait_recv()
+        for p in range(2):
+            onward(p, k, peer).start()
+
     def source(p, k, col):
         return inputs[p] if k == 0 else at(p, k, col)
 
     sends = []
     for k in range(DEPTH):
+        if k % 2 == 1 and k + 1 < DEPTH:
+            pl.when(first)(functools.partial(pass_on, k, first_next))
         if k > 0:
             for p in range(2):
                 remote(p, source(p, k, q), k, q, pred, relay_sem.at[k - 1]).wait_recv()
         if k + 1 < DEPTH:
-            for p in range(2):
-                cp = remote(p, source(p, k, q), k + 1, q, succ, relay_sem.at[k])
-                cp.start()
-                sends.append(cp)
+            via = last_next if k % 2 == 0 else first_here
+
+            @pl.when(jnp.logical_not(last))
+            def _():
+                for p in range(2):
+                    remote(p, source(p, k, q), k + 1, q, succ, relay_sem.at[k]).start()
+
+            @pl.when(last)
+            def _():
+                for p in range(2):
+                    to_hop(p, source(p, k, q), k, via).start()
+
+            if k % 2 == 0:
+                pl.when(last)(functools.partial(pass_on, k, first_here))
         for p in range(2):
             cp = remote(p, source(p, k, q), k, q, cross, cross_sem.at[k])
             cp.start()
@@ -147,6 +227,20 @@
 
     for cp in sends:
         cp.wait_send()
+    for k in range(DEPTH - 1):
+        for p in range(2):
+            remote(p, at(p, k, q), k + 1, q, succ, relay_sem.at[k]).wait_send()
+        if k % 2 == 0:
+            role = last
+            peer = first_here
+        else:
+            role = first
+            peer = first_next
+
+        @pl.when(role)
+        def _():
+            for p in range(2):
+                onward(p, k, peer).wait_send()
 
 
 def fused(block_docs, windows, key_rows, value_rows, q2, n_ctx, n_sub):
@@ -174,6 +268,10 @@
             pltpu.SemaphoreType.DMA((DEPTH, 2)),
             pltpu.SemaphoreType.DMA((DEPTH, 2)),
             pltpu.SemaphoreType.DMA((2,)),
+            pltpu.VMEM(((DEPTH - 1) * BLK, hd), key_rows.dtype),
+            pltpu.VMEM(((DEPTH - 1) * BLK, hd), value_rows.dtype),
+            pltpu.SemaphoreType.DMA((2, DEPTH - 1)),
+            pltpu.SemaphoreType.DMA((DEPTH - 1, 2)),
         ],
         compiler_params=pltpu.CompilerParams(
             collective_id=0, has_side_effects=True, vmem_limit_bytes=67043328

time: 66.8 us -> 69.8 us (1.045)
  the two profiles are of different devices: /device:TPU:63 before, /device:TPU:1 now
where the time goes in v9:
time: 69.8 us; the launch traced here: 69.7 us
  Pallas kernels  68 us (97%)
  local copies, waits for them, and re-layouts  1.67 us (2%)
    pallas_call x1, Pallas kernels, fused(): pl.pallas_call(functools.partial(fused_kernel, n_ctx, n_sub), out_shape=j...  68 us
    unnamed x1, local copies, waits for them, and re-layouts  1.67 us

profile of v9, /device:TPU:1, one launch (start us, length us, event | category | flops | bytes accessed | tf_op | source)
XLA Modules:
  0.0 69.7 jit_solution(13087352139261775138)
XLA Ops:
  0.0 68.0 %shard_map.55 = bf16[1024,128]{1,0:T(8,128)(2,1)} custom-call(s32[768]{0:T(1024)} %docs_hbm.1, s32[8]{0:T(128)} %win_hbm.1, bf16[128,128]{1,0:T(8,128)(2,1)} %k_ref.1, bf16[128,128]{1,0:T(8,128)(2,1)} %v_ref.1, bf16[1024,128]{1,0:T(8,128)(2,1)} %bitcast.3), custom_call_target="tpu_custom_call" | custom-call | tf_op jit(solution)/shard_map/pallas_call | solution.py:251
  68.0 1.7 %copy.7 = bf16[128,8,128]{2,1,0:T(8,128)(2,1)} copy(bf16[128,8,128]{2,1,0:T(8,128)(2,1)} %bitcast.2) | data formatting | bytes 524288

commit v10 on v8

--- a/solution.py
+++ b/solution.py
@@ -15,7 +15,7 @@
 
 
 def fused_kernel(n_ctx, n_sub, docs_hbm, win_hbm, k_ref, v_ref, q_hbm, out_ref,
-                 got_k, got_v, bias_sc, s_sc, q_ref, docs_ref, win_ref, in_sem,
+                 got_kv, bias_sc, s_sc, q_ref, docs_ref, win_ref, in_sem,
                  recv_sem, relay_sem, sib_sem, cross_sem, fwd_sem, own_sem):
     c = lax.axis_index("ctx")
     s = lax.axis_index("sub")
@@ -31,6 +31,8 @@
     far_q = 3 - q
     sib = (c, s - q + sib_q)
     cross = (c, s - q + cross_q)
+    got_k = got_kv.at[0]
+    got_v = got_kv.at[1]
     planes = (got_k, got_v)
     inputs = (k_ref, v_ref)
     rows, hd = q_ref.shape
@@ -40,6 +42,9 @@
 
     def at(p, k, col):
         return planes[p].at[pl.ds(pl.multiple_of((k * LEVEL + col) * BLK, BLK), BLK)]
+
+    def both(k, col):
+        return got_kv.at[:, pl.ds(pl.multiple_of((k * LEVEL + col) * BLK, BLK), BLK)]
 
     loads = [
         pltpu.make_async_copy(docs_hbm, docs_ref, in_sem.at[0]),
@@ -68,27 +73,50 @@
             device_id_type=MESH,
         )
 
+    def block(src_k, src_col, k, col, peer, sem):
+        return pltpu.make_async_remote_copy(
+            src_ref=both(src_k, src_col),
+            dst_ref=both(k, col),
+            send_sem=sem.at[0],
+            recv_sem=recv_sem.at[0, k, col],
+            device_id=peer,
+            device_id_type=MESH,
+        )
+
+    def send(k_src, col_src, k, col, peer, sem, out):
+        if k_src == 0 and col_src is q:
+            for p in range(2):
+                cp = remote(p, inputs[p], k, col, peer, sem)
+                cp.start()
+                out.append(cp)
+        else:
+            cp = block(k_src, col_src, k, col, peer, sem)
+            cp.start()
+            out.append(cp)
+
+    def arrive(k, col, peer, sem):
+        if k == 0 and col is q:
+            raise ValueError("own slot")
+        block(k, col, k, col, peer, sem).wait_recv()
+
+    def arrive_own_from(k, col, peer, sem, single):
+        if single:
+            for p in range(2):
+                remote(p, at(p, k, col), k, col, peer, sem).wait_recv()
+        else:
+            block(k, col, k, col, peer, sem).wait_recv()
+
     def source(p, k, col):
         return inputs[p] if k == 0 else at(p, k, col)
 
     sends = []
     for k in range(DEPTH):
         if k > 0:
-            for p in range(2):
-                remote(p, source(p, k, q), k, q, pred, relay_sem.at[k - 1]).wait_recv()
+            arrive_own_from(k, q, pred, relay_sem.at[k - 1], k == 1)
         if k + 1 < DEPTH:
-            for p in range(2):
-                cp = remote(p, source(p, k, q), k + 1, q, succ, relay_sem.at[k])
-                cp.start()
-                sends.append(cp)
-        for p in range(2):
-            cp = remote(p, source(p, k, q), k, q, cross, cross_sem.at[k])
-            cp.start()
-            sends.append(cp)
-        for p in range(2):
-            cp = remote(p, source(p, k, q), k, q, sib, sib_sem.at[k])
-            cp.start()
-            sends.append(cp)
+            send(k, q, k + 1, q, succ, relay_sem.at[k], sends)
+        send(k, q, k, q, cross, cross_sem.at[k], sends)
+        send(k, q, k, q, sib, sib_sem.at[k], sends)
         if k == 0:
             loads[0].wait()
             loads[1].wait()
@@ -106,18 +134,12 @@
                 bias_sc[:, pl.ds(slot * BLK, BLK)] = jnp.where(keep, 0.0, -jnp.inf).astype(jnp.float32)
 
     for k in range(DEPTH):
-        for p in range(2):
-            got_cross = at(p, k, cross_q)
-            remote(p, got_cross, k, cross_q, cross, cross_sem.at[k]).wait_recv()
-            cp = remote(p, got_cross, k, cross_q, sib, fwd_sem.at[k])
-            cp.start()
-            sends.append(cp)
+        arrive_own_from(k, cross_q, cross, cross_sem.at[k], k == 0)
+        send(k, cross_q, k, cross_q, sib, fwd_sem.at[k], sends)
 
     for k in range(DEPTH):
-        for p in range(2):
-            remote(p, at(p, k, sib_q), k, sib_q, sib, sib_sem.at[k]).wait_recv()
-        for p in range(2):
-            remote(p, at(p, k, far_q), k, far_q, sib, fwd_sem.at[k]).wait_recv()
+        arrive_own_from(k, sib_q, sib, sib_sem.at[k], k == 0)
+        arrive(k, far_q, sib, fwd_sem.at[k])
     for cp in owns:
         cp.wait()
     loads[2].wait()
@@ -160,8 +182,7 @@
         in_specs=[pl.BlockSpec(memory_space=pltpu.HBM)] * 5,
         out_specs=pl.BlockSpec(memory_space=pltpu.VMEM),
         scratch_shapes=[
-            pltpu.VMEM((keys, hd), key_rows.dtype),
-            pltpu.VMEM((keys, hd), value_rows.dtype),
+            pltpu.VMEM((2, keys, hd), key_rows.dtype),
             pltpu.VMEM((heads, keys), jnp.float32),
             pltpu.VMEM((chunk, keys), jnp.float32),
             pltpu.VMEM((rows, hd), q2.dtype),

time: 66.8 us -> 66.8 us (level)
  no operation moved by 1% of the time
where the time goes in v10:
time: 66.8 us; the launch traced here: 66.6 us
  Pallas kernels  64.9 us (97%)
  local copies, waits for them, and re-layouts  1.67 us (2%)
    pallas_call x1, Pallas kernels, fused(): pl.pallas_call(functools.partial(fused_kernel, n_ctx, n_sub), out_shape=j...  64.9 us
    unnamed x1, local copies, waits for them, and re-layouts  1.67 us

profile of v10, /device:TPU:63, one launch (start us, length us, event | category | flops | bytes accessed | tf_op | source)
XLA Modules:
  0.0 66.6 jit_solution(1235543119246237240)
XLA Ops:
  0.0 64.9 %shard_map.55 = bf16[1024,128]{1,0:T(8,128)(2,1)} custom-call(s32[768]{0:T(1024)} %docs_hbm.1, s32[8]{0:T(128)} %win_hbm.1, bf16[128,128]{1,0:T(8,128)(2,1)} %k_ref.1, bf16[128,128]{1,0:T(8,128)(2,1)} %v_ref.1, bf16[1024,128]{1,0:T(8,128)(2,1)} %bitcast.3), custom_call_target="tpu_custom_call" | custom-call | tf_op jit(solution)/shard_map/pallas_call | solution.py:179
  65.0 1.7 %copy.7 = bf16[128,8,128]{2,1,0:T(8,128)(2,1)} copy(bf16[128,8,128]{2,1,0:T(8,128)(2,1)} %bitcast.2) | data formatting | bytes 524288

commit v11 on v8

--- a/solution.py
+++ b/solution.py
@@ -152,7 +152,7 @@
 def fused(block_docs, windows, key_rows, value_rows, q2, n_ctx, n_sub):
     rows, hd = q2.shape
     keys = DEPTH * LEVEL * BLK
-    chunk = 256
+    chunk = 512
     heads = windows.shape[0]
     return pl.pallas_call(
         functools.partial(fused_kernel, n_ctx, n_sub),

time: 66.8 us -> 65.5 us (0.981)
  Pallas kernels: 65 us -> 63.7 us
    pallas_call x1, Pallas kernels: 65 us -> 63.7 us  [fused(): pl.pallas_call(functools.partial(fused_kernel, n_ctx, n_sub), out_shape=j...]
where the time goes in v11:
time: 65.5 us; the launch traced here: 65.4 us
  Pallas kernels  63.7 us (97%)
  local copies, waits for them, and re-layouts  1.67 us (3%)
    pallas_call x1, Pallas kernels, fused(): pl.pallas_call(functools.partial(fused_kernel, n_ctx, n_sub), out_shape=j...  63.7 us
    unnamed x1, local copies, waits for them, and re-layouts  1.67 us

profile of v11, /device:TPU:63, one launch (start us, length us, event | category | flops | bytes accessed | tf_op | source)
XLA Modules:
  0.0 65.4 jit_solution(552582918782697113)
XLA Ops:
  0.0 63.7 %shard_map.55 = bf16[1024,128]{1,0:T(8,128)(2,1)} custom-call(s32[768]{0:T(1024)} %docs_hbm.1, s32[8]{0:T(128)} %win_hbm.1, bf16[128,128]{1,0:T(8,128)(2,1)} %k_ref.1, bf16[128,128]{1,0:T(8,128)(2,1)} %v_ref.1, bf16[1024,128]{1,0:T(8,128)(2,1)} %bitcast.3), custom_call_target="tpu_custom_call" | custom-call | tf_op jit(solution)/shard_map/pallas_call | solution.py:157
  63.7 1.7 %copy.7 = bf16[128,8,128]{2,1,0:T(8,128)(2,1)} copy(bf16[128,8,128]{2,1,0:T(8,128)(2,1)} %bitcast.2) | data formatting | bytes 524288

commit v12 on v11

--- a/solution.py
+++ b/solution.py
@@ -152,7 +152,7 @@
 def fused(block_docs, windows, key_rows, value_rows, q2, n_ctx, n_sub):
     rows, hd = q2.shape
     keys = DEPTH * LEVEL * BLK
-    chunk = 512
+    chunk = 1024
     heads = windows.shape[0]
     return pl.pallas_call(
         functools.partial(fused_kernel, n_ctx, n_sub),

time: 65.5 us -> 64.8 us (0.989)
  Pallas kernels: 63.7 us -> 62.9 us
    pallas_call x1, Pallas kernels: 63.7 us -> 62.9 us  [fused(): pl.pallas_call(functools.partial(fused_kernel, n_ctx, n_sub), out_shape=j...]
where the time goes in v12:
time: 64.8 us; the launch traced here: 64.6 us
  Pallas kernels  62.9 us (97%)
  local copies, waits for them, and re-layouts  1.67 us (3%)
    pallas_call x1, Pallas kernels, fused(): pl.pallas_call(functools.partial(fused_kernel, n_ctx, n_sub), out_shape=j...  62.9 us
    unnamed x1, local copies, waits for them, and re-layouts  1.67 us

profile of v12, /device:TPU:63, one launch (start us, length us, event | category | flops | bytes accessed | tf_op | source)
XLA Modules:
  0.0 64.6 jit_solution(13623278737504613997)
XLA Ops:
  0.0 62.9 %shard_map.55 = bf16[1024,128]{1,0:T(8,128)(2,1)} custom-call(s32[768]{0:T(1024)} %docs_hbm.1, s32[8]{0:T(128)} %win_hbm.1, bf16[128,128]{1,0:T(8,128)(2,1)} %k_ref.1, bf16[128,128]{1,0:T(8,128)(2,1)} %v_ref.1, bf16[1024,128]{1,0:T(8,128)(2,1)} %bitcast.3), custom_call_target="tpu_custom_call" | custom-call | tf_op jit(solution)/shard_map/pallas_call | solution.py:157
  62.9 1.7 %copy.7 = bf16[128,8,128]{2,1,0:T(8,128)(2,1)} copy(bf16[128,8,128]{2,1,0:T(8,128)(2,1)} %bitcast.2) | data formatting | bytes 524288

commit v13 on v12

--- a/solution.py
+++ b/solution.py
@@ -124,7 +124,6 @@
 
     scale = hd ** -0.5
     own = pl.multiple_of(q * BLK, BLK)
-    ones = jnp.ones((keys, BLK), jnp.bfloat16)
 
     def one_chunk(ci, carry):
         r0 = pl.multiple_of(ci * chunk, chunk)
@@ -139,8 +138,8 @@
         m = jnp.max(sc, axis=1, keepdims=True)
         w = jnp.exp(sc - m).astype(jnp.bfloat16)
         num = jnp.dot(w, got_v[...], preferred_element_type=jnp.float32)
-        den = jnp.dot(w, ones, preferred_element_type=jnp.float32)
-        out_ref[pl.ds(r0, chunk), :] = (num / den[:, :1]).astype(out_ref.dtype)
+        den = jnp.sum(w.astype(jnp.float32), axis=1, keepdims=True)
+        out_ref[pl.ds(r0, chunk), :] = (num / den).astype(out_ref.dtype)
         return carry
 
     lax.fori_loop(0, rows // chunk, one_chunk, 0)

time: 64.8 us -> 70.1 us (1.082)
  Pallas kernels: 62.9 us -> 68.2 us
    pallas_call x1, Pallas kernels: 62.9 us -> 68.2 us  [fused(): pl.pallas_call(functools.partial(fused_kernel, n_ctx, n_sub), out_shape=j...]
where the time goes in v13:
time: 70.1 us; the launch traced here: 69.9 us
  Pallas kernels  68.2 us (97%)
  local copies, waits for them, and re-layouts  1.67 us (2%)
    pallas_call x1, Pallas kernels, fused(): pl.pallas_call(functools.partial(fused_kernel, n_ctx, n_sub), out_shape=j...  68.2 us
    unnamed x1, local copies, waits for them, and re-layouts  1.67 us

profile of v13, /device:TPU:63, one launch (start us, length us, event | category | flops | bytes accessed | tf_op | source)
XLA Modules:
  0.0 69.9 jit_solution(9602655752313571351)
XLA Ops:
  0.0 68.2 %shard_map.55 = bf16[1024,128]{1,0:T(8,128)(2,1)} custom-call(s32[768]{0:T(1024)} %docs_hbm.1, s32[8]{0:T(128)} %win_hbm.1, bf16[128,128]{1,0:T(8,128)(2,1)} %k_ref.1, bf16[128,128]{1,0:T(8,128)(2,1)} %v_ref.1, bf16[1024,128]{1,0:T(8,128)(2,1)} %bitcast.3), custom_call_target="tpu_custom_call" | custom-call | tf_op jit(solution)/shard_map/pallas_call | solution.py:156
  68.3 1.7 %copy.7 = bf16[128,8,128]{2,1,0:T(8,128)(2,1)} copy(bf16[128,8,128]{2,1,0:T(8,128)(2,1)} %bitcast.2) | data formatting | bytes 524288

commit v14 on v13

--- a/solution.py
+++ b/solution.py
@@ -15,7 +15,7 @@
 
 
 def fused_kernel(n_ctx, n_sub, docs_hbm, win_hbm, k_ref, v_ref, q_hbm, out_ref,
-                 got_k, got_v, bias_sc, s_sc, q_ref, docs_ref, win_ref, in_sem,
+                 got_k, got_v, bias_sc, s_sc, q_ref, docs_ref, win_ref, v_ones, in_sem,
                  recv_sem, relay_sem, sib_sem, cross_sem, fwd_sem, own_sem):
     c = lax.axis_index("ctx")
     s = lax.axis_index("sub")
@@ -121,6 +121,8 @@
     for cp in owns:
         cp.wait()
     loads[2].wait()
+    v_ones[:, :hd] = got_v[...]
+    v_ones[:, hd:] = jnp.ones((keys, BLK), got_v.dtype)
 
     scale = hd ** -0.5
     own = pl.multiple_of(q * BLK, BLK)
@@ -137,9 +139,8 @@
         sc = s_sc[...]
         m = jnp.max(sc, axis=1, keepdims=True)
         w = jnp.exp(sc - m).astype(jnp.bfloat16)
-        num = jnp.dot(w, got_v[...], preferred_element_type=jnp.float32)
-        den = jnp.sum(w.astype(jnp.float32), axis=1, keepdims=True)
-        out_ref[pl.ds(r0, chunk), :] = (num / den).astype(out_ref.dtype)
+        both = jnp.dot(w, v_ones[...], preferred_element_type=jnp.float32)
+        out_ref[pl.ds(r0, chunk), :] = (both[:, :hd] / both[:, hd:hd + 1]).astype(out_ref.dtype)
         return carry
 
     lax.fori_loop(0, rows // chunk, one_chunk, 0)
@@ -166,6 +167,7 @@
             pltpu.VMEM((rows, hd), q2.dtype),
             pltpu.SMEM(block_docs.shape, jnp.int32),
             pltpu.SMEM(windows.shape, jnp.int32),
+            pltpu.VMEM((keys, hd + BLK), value_rows.dtype),
             pltpu.SemaphoreType.DMA((3,)),
             pltpu.SemaphoreType.DMA((2, DEPTH, LEVEL)),
             pltpu.SemaphoreType.DMA((DEPTH, 2)),

time: 70.1 us -> 67.6 us (0.964)
  Pallas kernels: 68.2 us -> 65.8 us
    pallas_call x1, Pallas kernels: 68.2 us -> 65.8 us  [fused(): pl.pallas_call(functools.partial(fused_kernel, n_ctx, n_sub), out_shape=j...]
where the time goes in v14:
time: 67.6 us; the launch traced here: 67.4 us
  Pallas kernels  65.8 us (97%)
  local copies, waits for them, and re-layouts  1.67 us (2%)
    pallas_call x1, Pallas kernels, fused(): pl.pallas_call(functools.partial(fused_kernel, n_ctx, n_sub), out_shape=j...  65.8 us
    unnamed x1, local copies, waits for them, and re-layouts  1.67 us

profile of v14, /device:TPU:63, one launch (start us, length us, event | category | flops | bytes accessed | tf_op | source)
XLA Modules:
  0.0 67.4 jit_solution(13448094653567678674)
XLA Ops:
  0.0 65.8 %shard_map.55 = bf16[1024,128]{1,0:T(8,128)(2,1)} custom-call(s32[768]{0:T(1024)} %docs_hbm.1, s32[8]{0:T(128)} %win_hbm.1, bf16[128,128]{1,0:T(8,128)(2,1)} %k_ref.1, bf16[128,128]{1,0:T(8,128)(2,1)} %v_ref.1, bf16[1024,128]{1,0:T(8,128)(2,1)} %bitcast.3), custom_call_target="tpu_custom_call" | custom-call | tf_op jit(solution)/shard_map/pallas_call | solution.py:157
  65.8 1.7 %copy.7 = bf16[128,8,128]{2,1,0:T(8,128)(2,1)} copy(bf16[128,8,128]{2,1,0:T(8,128)(2,1)} %bitcast.2) | data formatting | bytes 524288
